TPU v7x, 512 devices: a whole 4x8x8 slice. The times are simulated.
512 devices in a mesh: row: 32 (over x, y), col: 16 (over z, core).
Axes of the slice: x: 4, y: 8, z: 8, core: 2. Of those that a mesh axis runs over, the one named last changes fastest.
Arguments:
- parent_sigma: float32 [4, 32, 128, 8, 16, 128], P(None, 'row', None, None, 'col'), as said below
- slot_tile: int32 [32, 2], replicated, may hold values from 0 to 3, as said below
- slot_count: int32 [32], replicated, may hold values from 1 to 2, as said below
- panel: float32 [32, 2, 128, 1024], P('row'), may hold values from -0.25 to 0.25
- sep_factor: float32 [1024, 1024], P('row'), as said below
Outputs:
- sigma_update: float32 [32, 2, 128, 1024], P('row')
- sigma_sep: float32 [1024, 1024], P('row')
Inputs may be any that keep to these rules, and one draw needn't show every extreme that they name: `parent_sigma`: symmetric when viewed as a [16384, 16384] matrix. `slot_tile`: the slots of one grid row name distinct tiles in increasing order. `slot_count`: every grid row has a live slot; some grid row has all 2 slots live. `sep_factor`: lower triangular with diagonal entries from 1.5 to 3.
All inputs are finite; a program needn't handle non-finite values.
Results may differ from a plain program's by a relative error of at most 0.00024.
Values sent between devices are 32-bit elements; how exact they have to be, the bound alone decides.
No kernel may reach another device: no remote copies, remote signals or barrier semaphores. Data moves between devices by JAX's collectives and lax.ppermute only.
A program may use at most 64 MiB of HBM per device.

v0:
```python
import jax
import jax.numpy as jnp
from jax import lax
from jax.sharding import PartitionSpec as P


def broadcast(shard, axis, root):
    mine = lax.axis_index(axis) == root
    return lax.psum(jnp.where(mine, shard, jnp.zeros_like(shard)), axis)


def exact_dot(left, right):
    return jnp.dot(left, right, precision=lax.Precision.HIGHEST, preferred_element_type=jnp.float32)


def lower_inverse(triangle):
    identity = jnp.eye(triangle.shape[0], dtype=jnp.float32)
    return jax.scipy.linalg.solve_triangular(triangle, identity, lower=True)


def combine_owners(owner_blocks, far_panels):
    partial_sum = exact_dot(owner_blocks[0], far_panels[0])
    partial_sum = partial_sum + exact_dot(owner_blocks[1], far_panels[1])
    return partial_sum


def column_total(partial_sum):
    return lax.psum(partial_sum, "col")


def row_total(stacked):
    return lax.psum(stacked, "row")


def on_device(parent_sigma, slot_tile, slot_count, panel, sep_factor):
    n_row = lax.axis_size("row")
    n_col = lax.axis_size("col")
    owner_ratio = n_row // n_col
    my_row = lax.axis_index("row")
    my_col = lax.axis_index("col")
    parent_rows = parent_sigma.shape[0]
    tile_size = parent_sigma.shape[2]
    parent_cols = parent_sigma.shape[3]
    slot_cap = panel.shape[1]
    sep_width = panel.shape[3]
    block_width = sep_width // 2
    local_sigma = parent_sigma.reshape(parent_rows, tile_size, parent_cols, tile_size)
    factor = lax.all_gather(sep_factor, "row", axis=0, tiled=True)
    first_inv = lower_inverse(factor[:block_width, :block_width])
    last_inv = lower_inverse(factor[block_width:, block_width:])
    coupling = exact_dot(factor[block_width:, :block_width], first_inv)
    live_slots = (jnp.arange(slot_cap, dtype=jnp.int32) < slot_count[my_row]).astype(jnp.float32)
    live_rows = jnp.repeat(live_slots, tile_size)[:, None]
    strips = panel.reshape(slot_cap * tile_size, sep_width) * live_rows
    first_u = exact_dot(strips[:, :block_width], first_inv)
    last_u = exact_dot(strips[:, block_width:], last_inv)
    own_block = jnp.take(local_sigma, slot_tile[my_row], axis=0)
    owner_blocks = []
    for owner_step in range(owner_ratio):
        columns = slot_tile[my_col + n_col * owner_step] * owner_ratio + owner_step
        picked = jnp.take(own_block, columns, axis=2)
        owner_blocks.append(picked.reshape(slot_cap * tile_size, slot_cap * tile_size))
    last_far = [
        broadcast(last_u, "row", my_col + n_col * owner_step) for owner_step in range(owner_ratio)
    ]
    last_partial = combine_owners(owner_blocks, last_far)
    last_y_part = column_total(last_partial) * live_rows
    inner_last = exact_dot(last_u.T, last_y_part)
    cross_part = -exact_dot(first_u.T, last_y_part)
    last_sums = row_total(jnp.stack([inner_last, cross_part]))
    sigma_last = exact_dot(last_inv.T, last_inv) + last_sums[0]
    cross_full = last_sums[1]
    first_far = [
        broadcast(first_u, "row", my_col + n_col * owner_step) for owner_step in range(owner_ratio)
    ]
    first_partial = combine_owners(owner_blocks, first_far)
    sigma_cross = exact_dot(sigma_last, coupling) + cross_full.T
    first_y = (column_total(first_partial) - exact_dot(last_y_part, coupling)) * live_rows
    first_sums = row_total(jnp.stack([exact_dot(first_u.T, first_y)]))
    sigma_first = (
        exact_dot(first_inv.T, first_inv) + first_sums[0] + exact_dot(coupling.T, sigma_cross)
    )
    update_block = -jnp.concatenate([first_y, last_y_part], axis=1)
    upper_rows = jnp.concatenate([sigma_first, -sigma_cross.T], axis=1)
    lower_rows = jnp.concatenate([-sigma_cross, sigma_last], axis=1)
    whole_sep = jnp.concatenate([upper_rows, lower_rows], axis=0)
    sep_rows = sep_width // n_row
    return (
        update_block.reshape(1, slot_cap, tile_size, sep_width),
        lax.dynamic_slice_in_dim(whole_sep, my_row * sep_rows, sep_rows, 0),
    )


def solution(mesh):
    placed = (
        P(None, "row", None, None, "col", None),
        P(),
        P(),
        P("row", None, None, None),
        P("row", None),
    )
    return jax.shard_map(
        on_device,
        mesh=mesh,
        in_specs=placed,
        out_specs=(P("row", None, None, None), P("row", None)),
        check_vma=False,
    )
```

profile of v0, /device:TPU:1, one launch (start us, length us, event | category | flops | bytes accessed | tf_op | source)
XLA Modules:
  0.0 718.6 jit_solution(6029491970669752011)
XLA Ops:
  10.1 2.4 bitcast_multiply_fusion
  12.5 88.6 %all-gather.2.cloned.1.call-done = f32[1024,1024]{1,0:T(8,128)} async-done(((f32[32,1024]{1,0:T(8,128)}), f32[1024,1024]{1,0:T(8,128)}) %all-gather.2.cloned.1.call-update) | async-done | bytes 4194320 | tf_op jit(solution)/shard_map/all_gather | solution.py:48
  101.1 3.2 slice_select_fusion.1
  104.3 11.9 %while.4 = (s32[]{:T(128)}, f32[512,512]{1,0:T(8,128)}, s32[4,2]{0,1:T(2,128)S(1)}, f32[4,128,128]{2,1,0:T(8,128)S(1)}, s32[]{:T(128)}) while((s32[]{:T(128)}, f32[512,512]{1,0:T(8,128)}, s32[4,2]{0,1:T(2,128)S(1)}, f32[4,128,128]{2,1,0:T(8,128)S(1)}, s32[]{:T(128)}) %tuple.56), condition=%wide.while_cond, body=%wide.while_body.sunk | while | flops 2 | bytes 131189 | solution.py:18
  105.0 2.3 bitcast_dynamic-update-slice_fusion.4
  107.9 2.3 bitcast_dynamic-update-slice_fusion.4
  110.9 2.3 bitcast_dynamic-update-slice_fusion.4
  113.9 2.2 bitcast_dynamic-update-slice_fusion.4
  116.2 39.9 %custom-call.4 = f32[4,128,128]{1,2,0:T(8,128)} custom-call(f32[4,128,128]{2,1,0:T(8,128)S(1)} %get-tuple-element.18), custom_call_target="InvertDiagBlocksLowerTriangular" | custom-call | tf_op jit(solution)/shard_map/jit(_solve_triangular)/triangular_solve | solution.py:18
  156.1 11.9 %while.5 = (s32[]{:T(128)}, f32[512,512]{1,0:T(8,128)}, s32[4,2]{0,1:T(2,128)S(1)}, f32[4,128,128]{2,1,0:T(8,128)S(1)}, s32[]{:T(128)}) while((s32[]{:T(128)}, f32[512,512]{1,0:T(8,128)}, s32[4,2]{0,1:T(2,128)S(1)}, f32[4,128,128]{2,1,0:T(8,128)S(1)}, s32[]{:T(128)}) %tuple.70), condition=%wide.while_cond.clone, body=%wide.while_body.clone.sunk | while | flops 2 | bytes 131189 | solution.py:18
  156.8 2.3 bitcast_dynamic-update-slice_fusion.5
  159.8 2.3 bitcast_dynamic-update-slice_fusion.5
  162.8 2.3 bitcast_dynamic-update-slice_fusion.5
  165.8 2.2 bitcast_dynamic-update-slice_fusion.5
  168.0 39.9 %custom-call.5 = f32[4,128,128]{1,2,0:T(8,128)} custom-call(f32[4,128,128]{2,1,0:T(8,128)S(1)} %get-tuple-element.19), custom_call_target="InvertDiagBlocksLowerTriangular" | custom-call | tf_op jit(solution)/shard_map/jit(_solve_triangular)/triangular_solve | solution.py:18
  222.8 2.3 broadcast_select_fusion.3
  225.1 2.2 broadcast_select_fusion.1
  234.0 154.9 %all-reduce.9.cloned.1.call-done = (f32[256,512]{1,0:T(8,128)}, f32[256,512]{1,0:T(8,128)}, f32[256,512]{1,0:T(8,128)}, f32[256,512]{1,0:T(8,128)}) async-done(((f32[256,512]{1,0:T(8,128)}, f32[256,512]{1,0:T(8,128)}, f32[256,512]{1,0:T(8,128)}, f32[256,512]{1,0:T(8,128)}), (f32[256,512]{1,0:T(8,128)}, f32[256,512]{1,0:T(8,128)}, f32[256,512]{1,0:T(8,128)}, ...) | async-done | bytes 2097168 | tf_op jit(solution)/shard_map/psum | solution.py:9
  388.9 1.7 fusion.32
  395.3 4.9 fusion.2
  400.2 114.9 %all-reduce.11.cloned.1.call-done = (f32[256,512]{1,0:T(8,128)}, f32[256,512]{1,0:T(8,128)}) async-done(((f32[256,512]{1,0:T(8,128)}, f32[256,512]{1,0:T(8,128)}), (f32[256,512]{1,0:T(8,128)}, f32[256,512]{1,0:T(8,128)})) %all-reduce.11.cloned.1.call-update) | async-done | bytes 1048592 | tf_op jit(solution)/shard_map/psum | solution.py:28
  516.4 2.3 convolution_bitcast_fusion
  521.6 2.1 fusion.74
  525.2 2.3 maximum_negate_fusion
  527.5 163.1 %all-reduce.7.cloned.1.call-done = (f32[512,512]{0,1:T(8,128)}, f32[2,512,512]{1,2,0:T(8,128)}) async-done(((f32[512,512]{0,1:T(8,128)}, f32[2,512,512]{1,2,0:T(8,128)}), (f32[512,512]{0,1:T(8,128)}, f32[2,512,512]{1,2,0:T(8,128)})) %all-reduce.7.cloned.1.call-update) | async-done | bytes 3145744 | tf_op jit(solution)/shard_map/psum | solution.py:32
  690.6 3.8 convolution_add_fusion.2
  694.4 1.9 convolution_add_fusion.1
  696.5 4.6 fusion.4
  702.4 2.9 convolution_add_fusion
  705.3 2.6 copy.24
  707.9 2.3 fusion.18
  710.2 1.9 copy.25
  (121 shorter events, 40.8 us)
Async XLA Ops:
  7.2 220.7 %copy-start = (f32[4,1,128,8,1,128]{5,4,3,2,1,0:T(1,128)S(1)}, f32[4,1,128,8,1,128]{5,4,3,2,1,0:T(1,128)}, u32[]{:S(2)}) copy-start(f32[4,1,128,8,1,128]{5,4,3,2,1,0:T(1,128)} %param.9) | copy-start | bytes 6291460
  7.2 93.9 %all-gather.2.cloned.1.call-start = ((), (), s32[]{:S(2)}) async-start(), calls=%async_computation | async-start | bytes 4325376 | tf_op jit(solution)/shard_map/all_gather | solution.py:48
  7.9 381.0 %all-reduce.9.cloned.1.call-start = ((), (), s32[]{:S(2)}) async-start(), calls=%async_computation.2 | async-start | bytes 4194304 | tf_op jit(solution)/shard_map/psum | solution.py:9
  208.0 6.6 copy-start.23
  210.5 14.6 %copy-start.5 = (f32[128,512]{1,0:T(8,128)}, f32[128,512]{1,0:T(8,128)S(1)}, u32[]{:S(2)}) copy-start(f32[128,512]{1,0:T(8,128)S(1)} %fusion.40) | copy-start | bytes 786436
  213.1 12.0 %copy-start.8 = (f32[128,512]{1,0:T(8,128)}, f32[128,512]{1,0:T(8,128)S(1)}, u32[]{:S(2)}) copy-start(f32[128,512]{1,0:T(8,128)S(1)} %fusion.51) | copy-start | bytes 786436
  213.1 5.3 copy-start.22
  215.0 10.1 %copy-start.14 = (f32[128,512]{1,0:T(8,128)}, f32[128,512]{1,0:T(8,128)S(1)}, u32[]{:S(2)}) copy-start(f32[128,512]{1,0:T(8,128)S(1)} %fusion.49) | copy-start | bytes 786436
  217.1 8.0 %copy-start.17 = (f32[128,512]{1,0:T(8,128)}, f32[128,512]{1,0:T(8,128)S(1)}, u32[]{:S(2)}) copy-start(f32[128,512]{1,0:T(8,128)S(1)} %fusion.48) | copy-start | bytes 786436
  218.4 4.4 copy-start.16
  218.8 6.3 copy-start.4
  220.7 4.4 copy-start.10
  222.8 4.6 copy-start.13
  225.1 2.5 copy-start.24
  227.4 287.7 %all-reduce.11.cloned.1.call-start = ((), (), s32[]{:S(2)}) async-start(), calls=%async_computation.3 | async-start | bytes 2097152 | tf_op jit(solution)/shard_map/psum | solution.py:28
  388.9 3.4 copy-start.20
  388.9 4.9 copy-start.19
  395.2 295.3 %all-reduce.7.cloned.1.call-start = ((), (), s32[]{:S(2)}) async-start(), calls=%async_computation.1 | async-start | bytes 6291456 | tf_op jit(solution)/shard_map/psum | solution.py:32
  515.2 3.5 copy-start.12
  516.4 3.4 copy-start.1
  516.4 3.4 copy-start.21
  520.9 0.8 copy-start.11
  690.6 3.8 copy-start.6
  690.6 3.8 copy-start.7
  690.6 3.8 copy-start.9
  690.6 3.8 copy-start.15
  690.6 3.8 copy-start.18
  696.5 4.6 copy-start.2
  705.3 2.6 copy-start.3
Sparse Core Ops, SparseCore 0:
  11.2 89.8 all-gather.1
  227.5 161.3 all-reduce.8
  395.4 119.7 all-reduce.10
  525.3 165.1 all-reduce.6
where the time goes:
time: 722 us; the launch traced here: 719 us
  waiting for transfers between devices  522 us (72%)
  other arithmetic  97.2 us (13%)
  matrix products  50 us (7%)
  local copies, waits for them, and re-layouts  34.1 us (5%)
  between operations  14.6 us (2%)
    psum x1, waiting for transfers between devices, row_total(): return lax.psum(stacked, 'row')  163 us
    psum x1, waiting for transfers between devices, broadcast(): return lax.psum(jnp.where(mine, shard, jnp.zeros_like(shard)), axis)  155 us
    psum x1, waiting for transfers between devices, column_total(): return lax.psum(partial_sum, 'col')  115 us
    all_gather x1, waiting for transfers between devices, on_device(): factor = lax.all_gather(sep_factor, 'row', axis=0, tiled=True)  88.6 us
    another operation x4, other arithmetic, lower_inverse(): return jax.scipy.linalg.solve_triangular(triangle, identity, lower=True)  83 us
    dot_general x15, matrix products, exact_dot(): jnp.dot(left, right, precision=lax.Precision.HIGHEST, preferred_element_t...  35.4 us
    another operation x27, local copies, waits for them, and re-layouts, lower_inverse(): return jax.scipy.linalg.solve_triangular(triangle, identity, lower=True)  23.7 us
    another operation x14, matrix products, lower_inverse(): return jax.scipy.linalg.solve_triangular(triangle, identity, lower=True)  14.6 us
  transfers between devices with their start and end apart: 4, of which 4 were waited for; matrix products, arithmetic and copies ran while one was open for 2% of the time, Pallas kernels for 0%

commit v1 on v0

v1 whole, which is shorter than its diff:
```python
import functools

import jax
import jax.numpy as jnp
import numpy as np
from jax import lax
from jax.experimental import pallas as pl
from jax.experimental.pallas import tpu as pltpu
from jax.sharding import Mesh
from jax.sharding import PartitionSpec as P

ROW = ("x", "y")
COL = ("z", "core")
X, Y, Z, CORE = 4, 8, 8, 2
N_ROW, N_COL = X * Y, Z * CORE
TILE = 128
SEP = 1024
STRIPE = SEP // X
PACKED = STRIPE * X * (X + 1) // 2
WIDTH = SEP // N_COL
OWN = SEP // N_ROW
LINES = OWN // N_COL
MIB = 1024 * 1024
HIGHEST = lax.Precision.HIGHEST


def exact_dot(left, right):
    return jnp.dot(left, right, precision=HIGHEST, preferred_element_type=jnp.float32)


def front_kernel(tile_ref, count_ref, me_ref, upper_ref, lower_ref, panel_ref, out_ref):
    row, col = me_ref[0], me_ref[1]
    live = [(slot < count_ref[row]).astype(jnp.float32) for slot in range(2)]
    strips = jnp.concatenate([panel_ref[0, slot] * live[slot] for slot in range(2)], axis=0)
    strips_t = strips.T
    for step in range(2):
        owner = col + N_COL * step
        block = jnp.concatenate(
            [
                jnp.concatenate(
                    [sigma[0, pl.ds(tile_ref[owner, slot] * 2 + step, TILE, stride=8), :] for slot in range(2)],
                    axis=1,
                )
                for sigma in (upper_ref, lower_ref)
            ],
            axis=0,
        )
        out_ref[step] = exact_dot(strips_t, block)


def front(slot_tile, slot_count, me, sigma, panel):
    def slab(slot):
        return pl.BlockSpec((1, TILE * 8, TILE), lambda i, tile, count, me: (tile[me[0], slot], 0, 0))

    return pl.pallas_call(
        front_kernel,
        grid_spec=pltpu.PrefetchScalarGridSpec(
            num_scalar_prefetch=3,
            grid=(1,),
            in_specs=[
                slab(0),
                slab(1),
                pl.BlockSpec((1, 2, TILE, SEP), lambda i, *_: (0, 0, 0, 0)),
            ],
            out_specs=pl.BlockSpec((2, SEP, 2 * TILE), lambda i, *_: (0, 0, 0)),
        ),
        out_shape=pltpu.VMEM((2, SEP, 2 * TILE), jnp.float32),
        compiler_params=pltpu.CompilerParams(vmem_limit_bytes=16 * MIB),
        name="front",
    )(slot_tile, slot_count, me, sigma, sigma, panel)


def invert_tiles(tiles):
    row = lax.broadcasted_iota(jnp.int32, (TILE, TILE), 0)
    col = lax.broadcasted_iota(jnp.int32, (TILE, TILE), 1)

    def left_of(size):
        return (row // (2 * size) == col // (2 * size)) & (row // size > col // size)

    inverses = []
    for tile in tiles:
        scale = jnp.where(row == col, 1.0 / jnp.where(row == col, tile, 1.0), 0.0)
        down = jnp.sum(scale, axis=1, keepdims=True)
        across = jnp.sum(scale, axis=0, keepdims=True)
        inverses.append(scale - jnp.where(left_of(1), tile * down * across, 0.0))
    size = 2
    while size < TILE:
        mask = left_of(size)
        products = [exact_dot(jnp.where(mask, tile, 0.0), inverse) for tile, inverse in zip(tiles, inverses)]
        inverses = [inverse - exact_dot(inverse, product) for inverse, product in zip(inverses, products)]
        size *= 2
    return inverses


def inverse_kernel(share_ref, out_ref, packed_ref):
    for block in range(PACKED // TILE):
        for y in range(Y):
            for line in range(LINES):
                start = (block * Y + y) * LINES + line
                taken = share_ref[pl.ds(start, N_COL, stride=PACKED // TILE * Y * LINES), :]
                packed_ref[block, pl.ds(y * OWN + line, N_COL, stride=LINES), :] = taken

    def factor(stripe, start, width):
        first = (STRIPE * stripe * (stripe + 1) // 2 + start) // TILE
        return jnp.concatenate([packed_ref[first + block] for block in range(width // TILE)], axis=1)

    diagonals = [factor(stripe, stripe * STRIPE, STRIPE) for stripe in range(X)]
    tiles = [d[p * TILE : (p + 1) * TILE, p * TILE : (p + 1) * TILE] for d in diagonals for p in range(2)]
    inverses = invert_tiles(tiles)
    middles = [exact_dot(d[TILE:, :TILE], inverses[2 * stripe]) for stripe, d in enumerate(diagonals)]
    corners = [-exact_dot(inverses[2 * stripe + 1], middle) for stripe, middle in enumerate(middles)]
    for stripe in range(X):
        top = stripe * STRIPE
        out_ref[top : top + TILE, top : top + TILE] = inverses[2 * stripe]
        out_ref[top : top + TILE, top + TILE :] = jnp.zeros((TILE, SEP - top - TILE), jnp.float32)
        out_ref[top + TILE : top + STRIPE, top : top + TILE] = corners[stripe]
        out_ref[top + TILE : top + STRIPE, top + TILE : top + STRIPE] = inverses[2 * stripe + 1]
        if stripe < X - 1:
            out_ref[top + TILE : top + STRIPE, top + STRIPE :] = jnp.zeros((TILE, SEP - top - STRIPE), jnp.float32)
    products = []
    for stripe in (1, 3):
        left = (stripe - 1) * STRIPE
        above = out_ref[left : left + STRIPE, left : left + STRIPE]
        products.append(exact_dot(factor(stripe, left, STRIPE), above))
    for stripe, product in zip((1, 3), products):
        top = stripe * STRIPE
        own = out_ref[top : top + STRIPE, top : top + STRIPE]
        out_ref[top : top + STRIPE, top - STRIPE : top] = -exact_dot(own, product)
    half = 2 * STRIPE
    left_part = jnp.concatenate([factor(2, 0, half), factor(3, 0, half)], axis=0)
    first_cols = exact_dot(left_part, out_ref[:half, :STRIPE])
    last_cols = exact_dot(left_part[:, STRIPE:], out_ref[STRIPE:half, STRIPE:half])
    product = jnp.concatenate([first_cols, last_cols], axis=1)
    out_ref[half : half + STRIPE, :half] = -exact_dot(out_ref[half : half + STRIPE, half : half + STRIPE], product[:STRIPE])
    out_ref[half + STRIPE :, :half] = -exact_dot(out_ref[half + STRIPE :, half:], product)


VMEM = pl.BlockSpec(memory_space=pltpu.VMEM)
SMEM = pl.BlockSpec(memory_space=pltpu.SMEM)


def on_chip(value):
    return pltpu.with_memory_space_constraint(value, pltpu.VMEM)


def factor_inverse(shares):
    return pl.pallas_call(
        inverse_kernel,
        in_specs=[VMEM],
        out_specs=VMEM,
        out_shape=pltpu.VMEM((SEP, SEP), jnp.float32),
        scratch_shapes=[pltpu.VMEM((PACKED // TILE, STRIPE, TILE), jnp.float32)],
        compiler_params=pltpu.CompilerParams(vmem_limit_bytes=20 * MIB),
        name="factor_inverse",
    )(shares)


def times_inverse(left, inverse_ref, stripe):
    start = stripe * STRIPE
    return exact_dot(left[:, start:], inverse_ref[start:, start : start + STRIPE])


def separator_kernel(me_ref, count_ref, piece_ref, panel_ref, inverse_ref, out_ref):
    row, col = me_ref[0], me_ref[1]
    live = [(slot < count_ref[row]).astype(jnp.float32) for slot in range(2)]
    strips = jnp.concatenate([panel_ref[0, slot] * live[slot] for slot in range(2)], axis=0)
    local = exact_dot(piece_ref[...], strips)
    down = lax.broadcasted_iota(jnp.int32, (WIDTH, SEP), 0) + col * WIDTH
    across = lax.broadcasted_iota(jnp.int32, (WIDTH, SEP), 1)
    local = local + jnp.where((down == across) & (row == 0), 1.0, 0.0)
    for stripe in range(X):
        turned = times_inverse(local, inverse_ref, stripe).T
        for place in range(STRIPE // OWN):
            start = place * OWN
            out_ref[stripe * (STRIPE // OWN) + place] = jnp.concatenate(
                [turned[start : start + OWN // 2], turned[start + OWN // 2 : start + OWN]], axis=1
            )


def separator(me, slot_count, piece, panel, inverse):
    return pl.pallas_call(
        separator_kernel,
        in_specs=[SMEM, SMEM, VMEM, VMEM, VMEM],
        out_specs=VMEM,
        out_shape=jax.ShapeDtypeStruct((N_ROW, OWN // 2, 2 * WIDTH), jnp.float32),
        compiler_params=pltpu.CompilerParams(vmem_limit_bytes=14 * MIB),
        name="separator",
    )(me, slot_count, piece, panel, on_chip(inverse))


def final_kernel(me_ref, count_ref, whole_ref, blocks_ref, inverse_ref, update_ref, sep_ref):
    row = me_ref[0]
    turned = whole_ref[...].T
    parts = [turned[slot * TILE : (slot + 1) * TILE] * -(slot < count_ref[row]).astype(jnp.float32) for slot in range(2)]
    for side in range(2):
        lanes = slice(side * WIDTH, (side + 1) * WIDTH)
        parts.append(jnp.concatenate([blocks_ref[place][:, lanes] for place in range(N_COL)], axis=1))
    left = jnp.concatenate(parts, axis=0)
    for stripe in range(X):
        lanes = slice(stripe * STRIPE, (stripe + 1) * STRIPE)
        result = times_inverse(left, inverse_ref, stripe)
        update_ref[0, 0, :, lanes] = result[:TILE]
        update_ref[0, 1, :, lanes] = result[TILE : 2 * TILE]
        sep_ref[:, lanes] = result[2 * TILE :]


def final(me, slot_count, whole, blocks, inverse):
    return pl.pallas_call(
        final_kernel,
        in_specs=[SMEM, SMEM, VMEM, VMEM, VMEM],
        out_specs=(VMEM, VMEM),
        out_shape=(
            jax.ShapeDtypeStruct((1, 2, TILE, SEP), jnp.float32),
            jax.ShapeDtypeStruct((OWN, SEP), jnp.float32),
        ),
        compiler_params=pltpu.CompilerParams(vmem_limit_bytes=14 * MIB),
        name="final",
    )(me, slot_count, whole, blocks, on_chip(inverse))


def total_kernel(pieces_ref, out_ref):
    out_ref[...] = jnp.sum(pieces_ref[...], axis=0)


def total(pieces):
    return pl.pallas_call(
        total_kernel,
        in_specs=[VMEM],
        out_specs=VMEM,
        out_shape=jax.ShapeDtypeStruct(pieces.shape[1:], jnp.float32),
        compiler_params=pltpu.CompilerParams(vmem_limit_bytes=8 * MIB),
        name="total",
    )(on_chip(pieces))


def spread(value, size):
    return jnp.broadcast_to(value[None], (size, *value.shape))


def exchange(blocks, axis):
    return lax.all_to_all(blocks, axis, 0, 0, tiled=True)


def spread_lines(sep_factor, col):
    return exchange(spread(lax.dynamic_slice_in_dim(sep_factor, col * LINES, LINES, 0), N_ROW), ROW)


def gather_factor(lines):
    stripes = lines.reshape(X, Y * LINES, SEP // TILE, TILE)
    count = STRIPE // TILE
    packed = jnp.concatenate([stripes[i, :, : count * (i + 1)].transpose(1, 0, 2) for i in range(X)], axis=0)
    return lax.all_gather(packed, COL, axis=0, tiled=True).reshape(-1, TILE)


def to_slot_owner():
    pairs = []
    for place in range(N_ROW):
        for col in range(N_COL):
            owner = col + N_COL * (place // N_COL)
            pairs.append((place * N_COL + col, owner * N_COL + place % N_COL))
    return pairs


def on_device(parent_sigma, slot_tile, slot_count, panel, sep_factor):
    my_row = lax.axis_index(ROW).astype(jnp.int32)
    my_col = lax.axis_index(COL).astype(jnp.int32)
    me = jnp.stack([my_row, my_col])
    sigma = parent_sigma.reshape(4, TILE * 8, TILE)
    with jax.named_scope("front_product"):
        partial = front(slot_tile, slot_count, me, sigma, panel).reshape(N_ROW, WIDTH, 2 * TILE)
    with jax.named_scope("factor_gather"):
        lines, partial = lax.optimization_barrier((spread_lines(sep_factor, my_col), partial))
        shares = gather_factor(lines)
    with jax.named_scope("inverse"):
        inverse = factor_inverse(shares)
    with jax.named_scope("front_sum"):
        pieces = exchange(partial, ROW)
        pieces, inverse = lax.optimization_barrier((pieces, inverse))
        piece = lax.ppermute(total(pieces), ROW + COL, to_slot_owner())
    with jax.named_scope("front_gather"):
        whole = lax.all_gather(piece, COL, axis=0, tiled=True)
    with jax.named_scope("separator"):
        sent = separator(me, slot_count, piece, panel, inverse)
        taken = total(exchange(sent, ROW))
        blocks = exchange(lax.optimization_barrier(spread(taken, N_COL)), COL)
    with jax.named_scope("final"):
        return final(me, slot_count, whole, blocks, inverse)


def solution(mesh):
    inner = Mesh(np.array(mesh.devices).reshape(X, Y, Z, CORE), ROW + COL)
    placed = (
        P(None, ROW, None, None, COL, None),
        P(),
        P(),
        P(ROW, None, None, None),
        P(ROW, None),
    )
    return jax.shard_map(
        on_device,
        mesh=inner,
        in_specs=placed,
        out_specs=(P(ROW, None, None, None), P(ROW, None)),
        check_vma=False,
    )
```

time: 722 us -> 165 us (0.23)
  waiting for transfers between devices: 522 us -> 43 us
  other arithmetic: 97.2 us -> 0.12 us
  matrix products: 50 us -> 0 us
  blocking collectives: 0 us -> 44 us
  starting transfers between devices: 0.34 us -> 22.4 us
  Pallas kernels: 0 us -> 21.6 us
  local copies, waits for them, and re-layouts: 34.1 us -> 19 us
    psum x3 -> x0, waiting for transfers between devices: 433 us -> none  [the longest x1 163 us: row_total(): return lax.psum(stacked, 'row')]
    another operation x5 -> x1, other arithmetic: 84.5 us -> 0.07 us  [on_device(): me = jnp.stack([my_row, my_col])]
    all_gather x1 -> x2, waiting for transfers between devices: 88.6 us -> 39.6 us  [the longest x1 39.6 us: gather_factor(): return lax.all_gather(packed, COL, axis=0, tiled=True).reshape(-1, TILE)]
    all_to_all x0 -> x2, blocking collectives: none -> 44 us  [exchange(): return lax.all_to_all(blocks, axis, 0, 0, tiled=True)]
    dot_general x15 -> x0, matrix products: 35.4 us -> none  [exact_dot(): jnp.dot(left, right, precision=lax.Precision.HIGHEST, preferred_element_t...]
    another operation x27 -> x0, local copies, waits for them, and re-layouts: 23.7 us -> none  [lower_inverse(): return jax.scipy.linalg.solve_triangular(triangle, identity, lower=True)]
    pallas_call x0 -> x6, Pallas kernels: none -> 21.6 us  [the longest x1 11.6 us: factor_inverse(): pl.pallas_call(inverse_kernel, in_specs=[VMEM], out_specs=VMEM, out_shape...]
    all_to_all x0 -> x2, starting transfers between devices: none -> 18.5 us  [exchange(): return lax.all_to_all(blocks, axis, 0, 0, tiled=True)]
  transfers between devices with their start and end apart: 4 -> 5, of which waited for: 4 -> 3; matrix products, arithmetic and copies ran while one was open for 2% -> 1% of each run, Pallas kernels for 0% -> 11%
where the time goes in v1:
time: 165 us; the launch traced here: 164 us
  blocking collectives  44 us (27%)
  waiting for transfers between devices  43 us (26%)
  starting transfers between devices  22.4 us (14%)
  Pallas kernels  21.6 us (13%)
  local copies, waits for them, and re-layouts  19 us (12%)
  between operations  14.2 us (9%)
    all_to_all x2, blocking collectives, exchange(): return lax.all_to_all(blocks, axis, 0, 0, tiled=True)  44 us
    all_gather x1, waiting for transfers between devices, gather_factor(): return lax.all_gather(packed, COL, axis=0, tiled=True).reshape(-1, TILE)  39.6 us
    all_to_all x2, starting transfers between devices, exchange(): return lax.all_to_all(blocks, axis, 0, 0, tiled=True)  18.5 us
    unnamed x29, local copies, waits for them, and re-layouts  17.2 us
    pallas_call x1, Pallas kernels, factor_inverse(): pl.pallas_call(inverse_kernel, in_specs=[VMEM], out_specs=VMEM, out_shape...  11.6 us
    pallas_call x1, Pallas kernels, final(): pl.pallas_call(final_kernel, in_specs=[SMEM, SMEM, VMEM, VMEM, VMEM], out...  4.23 us
    ppermute x1, starting transfers between devices, on_device(): piece = lax.ppermute(total(pieces), ROW + COL, to_slot_owner())  3.61 us
  transfers between devices with their start and end apart: 5, of which 3 were waited for; matrix products, arithmetic and copies ran while one was open for 1% of the time, Pallas kernels for 11%

profile of v1, /device:TPU:1, one launch (start us, length us, event | category | flops | bytes accessed | tf_op | source)
XLA Modules:
  0.0 164.3 jit_solution(9477347831573521390)
XLA Ops:
  7.2 0.9 copy-done
  8.1 0.8 broadcast_in_dim.4
  8.9 10.5 %all-to-all-start = ((f32[32,2,1024]{2,1,0:T(2,128)}), f32[32,2,1024]{2,1,0:T(2,128)S(1)}, u32[]{:S(2)}, u32[]{:S(2)}) async-start(f32[32,2,1024]{2,1,0:T(2,128)} %broadcast_in_dim.4), calls=%async_computation | async-start | bytes 524288 | tf_op jit(solution)/shard_map/factor_gather/all_to_all | solution.py:241
  19.4 0.8 copy.10.tile_ref
  20.2 0.1 pad_add_fusion.me_ref
  20.3 1.6 copy-done.5
  21.8 1.2 copy-done.6
  23.1 0.7 copy-done.12
  23.7 2.7 %front.1 = f32[2,1024,256]{2,1,0:T(8,128)S(1)} custom-call(s32[32,2]{1,0:T(8,128)S(1)} %copy.10.tile_ref, s32[32]{0:T(128)S(1)} %copy-done.12, s32[2]{0:T(128)S(1)} %pad_add_fusion.me_ref, f32[4,1024,128]{2,1,0:T(8,128)S(1)} %bitcast.19, f32[4,1024,128]{2,1,0:T(8,128)S(1)} %bitcast.20, f32[1,2,128,1024]{3,2,1,0:T(8,128)S(1)} %copy-done.6), custom_call_target="tpu_custom_call" | custom-call | tf_op jit(solution)/shard_map/front_product/front/pallas_call | solution.py:55
  26.5 1.3 copy-done.4
  27.8 1.3 all-to-all-done
  29.1 0.2 reshape.22
  29.3 0.1 squeeze.15
  29.4 0.7 copy.11
  30.2 8.0 %all-to-all-start.1 = ((f32[32,64,256]{2,1,0:T(8,128)}), f32[32,64,256]{2,1,0:T(8,128)S(1)}, u32[]{:S(2)}, u32[]{:S(2)}) async-start(f32[32,64,256]{2,1,0:T(8,128)} %bitcast.18), calls=%async_computation.1 | async-start | bytes 4194304 | tf_op jit(solution)/shard_map/front_sum/all_to_all | solution.py:241
  38.2 0.2 all-gather.5.cloned.1.call-start
  38.4 39.6 %all-gather.3.cloned.1.call-done = f32[320,16,128]{2,1,0:T(8,128)} async-done(((f32[20,16,128]{2,1,0:T(8,128)}), f32[320,16,128]{2,1,0:T(8,128)}) %all-gather.3.cloned.1.call-update) | async-done | bytes 2621456 | tf_op jit(solution)/shard_map/factor_gather/all_gather | solution.py:252
  78.0 1.7 %copy-done.8 = f32[320,16,128]{2,1,0:T(8,128)S(1)} copy-done((f32[320,16,128]{2,1,0:T(8,128)S(1)}, f32[320,16,128]{2,1,0:T(8,128)}, u32[]{:S(2)}) %copy-start.8) | copy-done | bytes 2621464
  79.7 11.6 %factor_inverse.1.inverse_ref = f32[1024,1024]{1,0:T(8,128)S(1)} custom-call(f32[5120,128]{1,0:T(8,128)S(1)} %bitcast.21), custom_call_target="tpu_custom_call" | custom-call | tf_op jit(solution)/shard_map/inverse/factor_inverse/pallas_call | solution.py:147
  91.3 1.9 %copy-done.1 = f32[1024,1024]{1,0:T(8,128)} copy-done((f32[1024,1024]{1,0:T(8,128)}, f32[1024,1024]{1,0:T(8,128)S(1)}, u32[]{:S(2)}) %copy-start.1) | copy-done | bytes 4194328
  93.3 0.1 total.2
  93.4 3.6 %collective-permute-start = (f32[64,256]{1,0:T(8,128)S(1)}, f32[64,256]{1,0:T(8,128)S(1)}, u32[]{:S(2)}, u32[]{:S(2)}) collective-permute-start(f32[64,256]{1,0:T(8,128)S(1)} %total.2), channel_id=1, source_target_pairs={{0,0},{1,16},{2,32},{3,48},{4,64},{5,80},{6,96},{7,112},{8,128},{9... | collective-permute-start | bytes 196616 | tf_op jit(solution)/shard_map/front_sum/ppermute | solution.py:279
  97.0 2.1 %collective-permute-done.piece_ref = f32[64,256]{1,0:T(8,128)S(1)} collective-permute-done((f32[64,256]{1,0:T(8,128)S(1)}, f32[64,256]{1,0:T(8,128)S(1)}, u32[]{:S(2)}, u32[]{:S(2)}) %collective-permute-start) | collective-permute-done | bytes 65568 | tf_op jit(solution)/shard_map/front_sum/ppermute | solution.py:279
  99.1 0.6 copy-done.10
  99.8 2.2 %copy-done.2 = f32[1024,1024]{1,0:T(8,128)S(1)} copy-done((f32[1024,1024]{1,0:T(8,128)S(1)}, f32[1024,1024]{1,0:T(8,128)}, u32[]{:S(2)}) %copy-start.2) | copy-done | bytes 4194328
  102.0 0.8 copy-done.11
  102.8 2.9 %separator.1 = f32[32,16,128]{2,1,0:T(8,128)S(1)} custom-call(s32[2]{0:T(128)S(1)} %pad_add_fusion.me_ref, s32[32]{0:T(128)S(1)} %copy-done.13, f32[64,256]{1,0:T(8,128)S(1)} %copy-done.11, f32[1,2,128,1024]{3,2,1,0:T(8,128)S(1)} %copy-done.7, f32[1024,1024]{1,0:T(8,128)S(1)} %copy-done.2), custom_call_target="tpu_custom_call" | custom-call | tf_op jit(solution)/shard_map/separator/separator/pallas_call | solution.py:181
  105.8 25.5 %all_to_all.20.pieces_ref = f32[32,16,128]{2,1,0:T(8,128)S(1)} all-to-all(f32[32,16,128]{2,1,0:T(8,128)S(1)} %separator.1), channel_id=1, replica_groups=mesh['x'=4,'y'=8,'z'=8,'core'=2] {'x','y'}, dimensions={0} | all-to-all | bytes 524288 | tf_op jit(solution)/shard_map/separator/all_to_all | solution.py:241
  131.4 18.5 %all_to_all.21.blocks_ref = f32[16,16,128]{2,1,0:T(8,128)S(1)} all-to-all(f32[16,16,128]{2,1,0:T(8,128)S(1)} %broadcast_in_dim.5), channel_id=1, replica_groups=mesh['x'=4,'y'=8,'z'=8,'core'=2] {'z','core'}, dimensions={0} | all-to-all | bytes 262144 | tf_op jit(solution)/shard_map/separator/all_to_all | solution.py:241
  149.8 2.2 %copy-done.3 = f32[1024,1024]{1,0:T(8,128)S(1)} copy-done((f32[1024,1024]{1,0:T(8,128)S(1)}, f32[1024,1024]{1,0:T(8,128)}, u32[]{:S(2)}) %copy-start.3) | copy-done | bytes 4194328
  152.0 1.2 copy-done.9
  153.3 4.2 %final.1 = (f32[1,2,128,1024]{3,2,1,0:T(8,128)}, f32[32,1024]{1,0:T(8,128)}) custom-call(s32[2]{0:T(128)S(1)} %pad_add_fusion.me_ref, s32[32]{0:T(128)S(1)} %copy-done.13, f32[1024,256]{1,0:T(8,128)S(1)} %copy-done.9, f32[16,16,128]{2,1,0:T(8,128)S(1)} %all_to_all.21.blocks_ref, f32[1024,1024]{1,0:T(8,128)S(1)} %copy-done.3), custom_call_target="tpu_custom_call" | custom-call | tf_op jit(solution)/shard_map/final/final/pallas_call | solution.py:208
  (29 shorter events, 0.2 us)
Async XLA Ops:
  7.2 0.9 copy-start
  8.9 20.2 %all-to-all-start = ((f32[32,2,1024]{2,1,0:T(2,128)}), f32[32,2,1024]{2,1,0:T(2,128)S(1)}, u32[]{:S(2)}, u32[]{:S(2)}) async-start(f32[32,2,1024]{2,1,0:T(2,128)} %broadcast_in_dim.4), calls=%async_computation | async-start | bytes 524288 | tf_op jit(solution)/shard_map/factor_gather/all_to_all | solution.py:241
  19.4 58.6 %all-gather.3.cloned.1.call-start = ((), (), s32[]{:S(2)}) async-start(), calls=%async_computation.4 | async-start | bytes 2785280 | tf_op jit(solution)/shard_map/factor_gather/all_gather | solution.py:252
  20.3 1.6 copy-start.5
  21.8 1.2 copy-start.6
  23.1 0.7 copy-start.12
  26.5 1.3 copy-start.4
  30.2 63.1 %all-to-all-start.1 = ((f32[32,64,256]{2,1,0:T(8,128)}), f32[32,64,256]{2,1,0:T(8,128)S(1)}, u32[]{:S(2)}, u32[]{:S(2)}) async-start(f32[32,64,256]{2,1,0:T(8,128)} %bitcast.18), calls=%async_computation.1 | async-start | bytes 4194304 | tf_op jit(solution)/shard_map/front_sum/all_to_all | solution.py:241
  38.2 111.7 %all-gather.5.cloned.1.call-start = ((), (), s32[]{:S(2)}) async-start(), calls=%async_computation.5 | async-start | bytes 1114112 | tf_op jit(solution)/shard_map/front_gather/all_gather | solution.py:281
  78.0 1.7 %copy-start.8 = (f32[320,16,128]{2,1,0:T(8,128)S(1)}, f32[320,16,128]{2,1,0:T(8,128)}, u32[]{:S(2)}) copy-start(f32[320,16,128]{2,1,0:T(8,128)} %all-gather.3.cloned.1.call-done) | copy-start | bytes 7864324
  91.3 1.9 %copy-start.1 = (f32[1024,1024]{1,0:T(8,128)}, f32[1024,1024]{1,0:T(8,128)S(1)}, u32[]{:S(2)}) copy-start(f32[1024,1024]{1,0:T(8,128)S(1)} %factor_inverse.1.inverse_ref) | copy-start | bytes 12582916
  93.3 6.5 %copy-start.7 = (f32[1,2,128,1024]{3,2,1,0:T(8,128)S(1)}, f32[1,2,128,1024]{3,2,1,0:T(8,128)}, u32[]{:S(2)}) copy-start(f32[1,2,128,1024]{3,2,1,0:T(8,128)} %panel_ref.3) | copy-start | bytes 3145732
  93.3 6.5 %copy-start.13 = (s32[32]{0:T(128)S(1)}, s32[32]{0:T(128)}, u32[]{:S(2)}) copy-start(s32[32]{0:T(128)} %count_ref.5) | copy-start | bytes 388
  93.4 5.7 %collective-permute-start = (f32[64,256]{1,0:T(8,128)S(1)}, f32[64,256]{1,0:T(8,128)S(1)}, u32[]{:S(2)}, u32[]{:S(2)}) collective-permute-start(f32[64,256]{1,0:T(8,128)S(1)} %total.2), channel_id=1, source_target_pairs={{0,0},{1,16},{2,32},{3,48},{4,64},{5,80},{6,96},{7,112},{8,128},{9... | collective-permute-start | bytes 196616 | tf_op jit(solution)/shard_map/front_sum/ppermute | solution.py:279
  99.1 0.6 copy-start.10
  99.8 2.2 %copy-start.2 = (f32[1024,1024]{1,0:T(8,128)S(1)}, f32[1024,1024]{1,0:T(8,128)}, u32[]{:S(2)}) copy-start(f32[1024,1024]{1,0:T(8,128)} %copy-done.1) | copy-start | bytes 12582916
  102.0 0.8 copy-start.11
  149.8 2.2 %copy-start.3 = (f32[1024,1024]{1,0:T(8,128)S(1)}, f32[1024,1024]{1,0:T(8,128)}, u32[]{:S(2)}) copy-start(f32[1024,1024]{1,0:T(8,128)} %copy-done.1) | copy-start | bytes 12582916
  152.0 1.2 copy-start.9
Sparse Core Ops, SparseCore 0:
  30.3 47.6 all-gather.2
  99.9 48.8 all-gather.4

commit v2 on v1

--- a/solution.py
+++ b/solution.py
@@ -26,6 +26,14 @@
 
 def exact_dot(left, right):
     return jnp.dot(left, right, precision=HIGHEST, preferred_element_type=jnp.float32)
+
+
+def on_chip(value):
+    return pltpu.with_memory_space_constraint(value, pltpu.VMEM)
+
+
+def off_chip(value):
+    return pltpu.with_memory_space_constraint(value, pltpu.HBM)
 
 
 def front_kernel(tile_ref, count_ref, me_ref, upper_ref, lower_ref, panel_ref, out_ref):
@@ -64,10 +72,10 @@
             ],
             out_specs=pl.BlockSpec((2, SEP, 2 * TILE), lambda i, *_: (0, 0, 0)),
         ),
-        out_shape=pltpu.VMEM((2, SEP, 2 * TILE), jnp.float32),
+        out_shape=jax.ShapeDtypeStruct((2, SEP, 2 * TILE), jnp.float32),
         compiler_params=pltpu.CompilerParams(vmem_limit_bytes=16 * MIB),
         name="front",
-    )(slot_tile, slot_count, me, sigma, sigma, panel)
+    )(slot_tile, slot_count, me, off_chip(sigma), off_chip(sigma), off_chip(panel))
 
 
 def invert_tiles(tiles):
@@ -139,25 +147,30 @@
 SMEM = pl.BlockSpec(memory_space=pltpu.SMEM)
 
 
-def on_chip(value):
-    return pltpu.with_memory_space_constraint(value, pltpu.VMEM)
-
-
 def factor_inverse(shares):
     return pl.pallas_call(
         inverse_kernel,
         in_specs=[VMEM],
         out_specs=VMEM,
-        out_shape=pltpu.VMEM((SEP, SEP), jnp.float32),
+        out_shape=jax.ShapeDtypeStruct((SEP, SEP), jnp.float32),
         scratch_shapes=[pltpu.VMEM((PACKED // TILE, STRIPE, TILE), jnp.float32)],
         compiler_params=pltpu.CompilerParams(vmem_limit_bytes=20 * MIB),
         name="factor_inverse",
     )(shares)
 
 
-def times_inverse(left, inverse_ref, stripe):
+def times_inverse(left_ref, inverse_ref, stripe):
     start = stripe * STRIPE
-    return exact_dot(left[:, start:], inverse_ref[start:, start : start + STRIPE])
+    return exact_dot(left_ref[:, start:], inverse_ref[start:, :])
+
+
+def for_stripe(body):
+    for stripe in range(X):
+        pl.when(pl.program_id(0) == stripe)(functools.partial(body, stripe))
+
+
+def whole_block(shape):
+    return pl.BlockSpec(shape, lambda i: (0,) * len(shape))
 
 
 def separator_kernel(me_ref, count_ref, piece_ref, panel_ref, inverse_ref, out_ref):
@@ -169,7 +182,8 @@
     across = lax.broadcasted_iota(jnp.int32, (WIDTH, SEP), 1)
     local = local + jnp.where((down == across) & (row == 0), 1.0, 0.0)
     for stripe in range(X):
-        turned = times_inverse(local, inverse_ref, stripe).T
+        first = stripe * STRIPE
+        turned = exact_dot(local[:, first:], inverse_ref[first:, first : first + STRIPE]).T
         for place in range(STRIPE // OWN):
             start = place * OWN
             out_ref[stripe * (STRIPE // OWN) + place] = jnp.concatenate(
@@ -185,37 +199,55 @@
         out_shape=jax.ShapeDtypeStruct((N_ROW, OWN // 2, 2 * WIDTH), jnp.float32),
         compiler_params=pltpu.CompilerParams(vmem_limit_bytes=14 * MIB),
         name="separator",
-    )(me, slot_count, piece, panel, on_chip(inverse))
-
-
-def final_kernel(me_ref, count_ref, whole_ref, blocks_ref, inverse_ref, update_ref, sep_ref):
-    row = me_ref[0]
-    turned = whole_ref[...].T
-    parts = [turned[slot * TILE : (slot + 1) * TILE] * -(slot < count_ref[row]).astype(jnp.float32) for slot in range(2)]
-    for side in range(2):
-        lanes = slice(side * WIDTH, (side + 1) * WIDTH)
-        parts.append(jnp.concatenate([blocks_ref[place][:, lanes] for place in range(N_COL)], axis=1))
-    left = jnp.concatenate(parts, axis=0)
-    for stripe in range(X):
-        lanes = slice(stripe * STRIPE, (stripe + 1) * STRIPE)
-        result = times_inverse(left, inverse_ref, stripe)
-        update_ref[0, 0, :, lanes] = result[:TILE]
-        update_ref[0, 1, :, lanes] = result[TILE : 2 * TILE]
-        sep_ref[:, lanes] = result[2 * TILE :]
+    )(me, slot_count, piece, panel, inverse)
+
+
+def final_kernel(me_ref, count_ref, whole_ref, blocks_ref, inverse_ref, update_ref, sep_ref, left_ref):
+    @pl.when(pl.program_id(0) == 0)
+    def _():
+        row = me_ref[0]
+        turned = whole_ref[...].T
+        for slot in range(2):
+            sign = -(slot < count_ref[row]).astype(jnp.float32)
+            left_ref[slot * TILE : (slot + 1) * TILE, :] = turned[slot * TILE : (slot + 1) * TILE] * sign
+        for side in range(2):
+            lanes = slice(side * WIDTH, (side + 1) * WIDTH)
+            start = 2 * TILE + side * (OWN // 2)
+            left_ref[start : start + OWN // 2, :] = jnp.concatenate(
+                [blocks_ref[place][:, lanes] for place in range(N_COL)], axis=1
+            )
+
+    @for_stripe
+    def _(stripe):
+        result = times_inverse(left_ref, inverse_ref, stripe)
+        update_ref[0, 0] = result[:TILE]
+        update_ref[0, 1] = result[TILE : 2 * TILE]
+        sep_ref[...] = result[2 * TILE :]
 
 
 def final(me, slot_count, whole, blocks, inverse):
     return pl.pallas_call(
         final_kernel,
-        in_specs=[SMEM, SMEM, VMEM, VMEM, VMEM],
-        out_specs=(VMEM, VMEM),
+        grid=(X,),
+        in_specs=[
+            SMEM,
+            SMEM,
+            whole_block((SEP, 2 * TILE)),
+            whole_block((N_COL, OWN // 2, 2 * WIDTH)),
+            pl.BlockSpec((SEP, STRIPE), lambda i: (0, i)),
+        ],
+        out_specs=(
+            pl.BlockSpec((1, 2, TILE, STRIPE), lambda i: (0, 0, 0, i)),
+            pl.BlockSpec((OWN, STRIPE), lambda i: (0, i)),
+        ),
         out_shape=(
             jax.ShapeDtypeStruct((1, 2, TILE, SEP), jnp.float32),
             jax.ShapeDtypeStruct((OWN, SEP), jnp.float32),
         ),
-        compiler_params=pltpu.CompilerParams(vmem_limit_bytes=14 * MIB),
+        scratch_shapes=[pltpu.VMEM((2 * TILE + OWN, SEP), jnp.float32)],
+        compiler_params=pltpu.CompilerParams(vmem_limit_bytes=16 * MIB),
         name="final",
-    )(me, slot_count, whole, blocks, on_chip(inverse))
+    )(me, slot_count, off_chip(whole), blocks, off_chip(inverse))
 
 
 def total_kernel(pieces_ref, out_ref):
@@ -271,14 +303,15 @@
     with jax.named_scope("factor_gather"):
         lines, partial = lax.optimization_barrier((spread_lines(sep_factor, my_col), partial))
         shares = gather_factor(lines)
-    with jax.named_scope("inverse"):
-        inverse = factor_inverse(shares)
     with jax.named_scope("front_sum"):
-        pieces = exchange(partial, ROW)
-        pieces, inverse = lax.optimization_barrier((pieces, inverse))
-        piece = lax.ppermute(total(pieces), ROW + COL, to_slot_owner())
+        half = total(exchange(partial.reshape(X, Y, WIDTH, 2 * TILE), "x"))
+        piece = total(exchange(half, "y"))
+        piece = lax.ppermute(piece, ROW + COL, to_slot_owner())
     with jax.named_scope("front_gather"):
         whole = lax.all_gather(piece, COL, axis=0, tiled=True)
+    with jax.named_scope("inverse"):
+        shares, _ = lax.optimization_barrier((shares, piece))
+        inverse = factor_inverse(shares)
     with jax.named_scope("separator"):
         sent = separator(me, slot_count, piece, panel, inverse)
         taken = total(exchange(sent, ROW))

time: 165 us -> 159 us (0.964)
  waiting for transfers between devices: 43 us -> 15.5 us
  blocking collectives: 44 us -> 69.3 us
  local copies, waits for them, and re-layouts: 19 us -> 7.14 us
  starting transfers between devices: 22.4 us -> 27 us
  Pallas kernels: 21.6 us -> 25.7 us
    all_gather x1, waiting for transfers between devices: 39.6 us -> 0.02 us  [gather_factor(): return lax.all_gather(packed, COL, axis=0, tiled=True).reshape(-1, TILE)]
    all_to_all x2 -> x3, blocking collectives: 44 us -> 69.3 us  [exchange(): return lax.all_to_all(blocks, axis, 0, 0, tiled=True)]
    unnamed x29 -> x17, local copies, waits for them, and re-layouts: 17.2 us -> 4.71 us
    all_to_all x2, waiting for transfers between devices: 1.25 us -> 13 us  [exchange(): return lax.all_to_all(blocks, axis, 0, 0, tiled=True)]
    ppermute x1, starting transfers between devices: 3.61 us -> 7.02 us  [on_device(): piece = lax.ppermute(piece, ROW + COL, to_slot_owner())]
    pallas_call x1, Pallas kernels: 4.23 us -> 6.46 us  [final(): pl.pallas_call(final_kernel, grid=(X,), in_specs=[SMEM, SMEM, whole_block...]
  transfers between devices with their start and end apart: 5 -> 5, of which waited for: 3 -> 3; matrix products, arithmetic and copies ran while one was open for 1% -> 1% of each run, Pallas kernels for 11% -> 12%
where the time goes in v2:
time: 159 us
  blocking collectives  69.3 us (44%)
  starting transfers between devices  27 us (17%)
  Pallas kernels  25.7 us (16%)
  waiting for transfers between devices  15.5 us (10%)
  between operations  14.2 us (9%)
  local copies, waits for them, and re-layouts  7.14 us (4%)
    all_to_all x3, blocking collectives, exchange(): return lax.all_to_all(blocks, axis, 0, 0, tiled=True)  69.3 us
    all_to_all x2, starting transfers between devices, exchange(): return lax.all_to_all(blocks, axis, 0, 0, tiled=True)  19.9 us
    all_to_all x2, waiting for transfers between devices, exchange(): return lax.all_to_all(blocks, axis, 0, 0, tiled=True)  13 us
    pallas_call x1, Pallas kernels, factor_inverse(): pl.pallas_call(inverse_kernel, in_specs=[VMEM], out_specs=VMEM, out_shape...  11.6 us
    ppermute x1, starting transfers between devices, on_device(): piece = lax.ppermute(piece, ROW + COL, to_slot_owner())  7.02 us
    pallas_call x1, Pallas kernels, final(): pl.pallas_call(final_kernel, grid=(X,), in_specs=[SMEM, SMEM, whole_block...  6.46 us
    unnamed x17, local copies, waits for them, and re-layouts  4.71 us
    pallas_call x1, Pallas kernels, front(): pl.pallas_call(front_kernel, grid_spec=pltpu.PrefetchScalarGridSpec(num_s...  4.27 us
  transfers between devices with their start and end apart: 5, of which 3 were waited for; matrix products, arithmetic and copies ran while one was open for 1% of the time, Pallas kernels for 12%

profile of v2, /device:TPU:1, one launch (start us, length us, event | category | flops | bytes accessed | tf_op | source)
XLA Modules:
  0.0 158.9 jit_solution(2970781108104905157)
XLA Ops:
  7.2 0.0 copy-start
  7.2 0.9 copy-done
  8.1 0.8 broadcast_in_dim.4
  8.9 10.5 %all-to-all-start = ((f32[32,2,1024]{2,1,0:T(2,128)}), f32[32,2,1024]{2,1,0:T(2,128)S(1)}, u32[]{:S(2)}, u32[]{:S(2)}) async-start(f32[32,2,1024]{2,1,0:T(2,128)} %broadcast_in_dim.4), calls=%async_computation | async-start | bytes 524288 | tf_op jit(solution)/shard_map/factor_gather/all_to_all | solution.py:273
  19.4 0.0 all-gather.5.cloned.1.call-start
  19.4 0.8 copy.10.tile_ref
  20.2 0.1 pad_add_fusion.me_ref
  20.3 0.7 copy-done.6
  20.9 4.3 %front.1 = f32[2,1024,256]{2,1,0:T(8,128)S(1)} custom-call(s32[32,2]{1,0:T(8,128)S(1)} %copy.10.tile_ref, s32[32]{0:T(128)S(1)} %copy-done.6, s32[2]{0:T(128)S(1)} %pad_add_fusion.me_ref, f32[4,1024,128]{2,1,0:T(8,128)} %bitcast.21, f32[4,1024,128]{2,1,0:T(8,128)} %bitcast.22, f32[1,2,128,1024]{3,2,1,0:T(8,128)} %panel_ref.3), custom_call_target="tpu_custom_call" | custom-call | tf_op jit(solution)/shard_map/front_product/front/pallas_call | solution.py:63
  25.2 3.9 %all-to-all-done = f32[32,2,1024]{2,1,0:T(2,128)S(1)} async-done(((f32[32,2,1024]{2,1,0:T(2,128)}), f32[32,2,1024]{2,1,0:T(2,128)S(1)}, u32[]{:S(2)}, u32[]{:S(2)}) %all-to-all-start) | async-done | bytes 262176 | tf_op jit(solution)/shard_map/factor_gather/all_to_all | solution.py:273
  29.1 0.2 reshape.26
  29.3 0.1 squeeze.15
  29.4 0.7 copy.11
  30.1 0.0 all-gather.5.cloned.1.call-update
  30.2 0.0 all-gather.3.cloned.1.call-start
  30.2 25.1 %all_to_all.25.pieces_ref = f32[4,8,64,256]{3,2,1,0:T(8,128)S(1)} all-to-all(f32[4,8,64,256]{3,2,1,0:T(8,128)S(1)} %bitcast.19), channel_id=1, replica_groups=mesh['x'=4,'y'=8,'z'=8,'core'=2] {'x'}, dimensions={0} | all-to-all | bytes 4194304 | tf_op jit(solution)/shard_map/front_sum/all_to_all | solution.py:273
  55.3 0.1 total.3
  55.4 20.2 %all_to_all.26.pieces_ref = f32[8,64,256]{2,1,0:T(8,128)S(1)} all-to-all(f32[8,64,256]{2,1,0:T(8,128)S(1)} %total.3), channel_id=1, replica_groups=mesh['x'=4,'y'=8,'z'=8,'core'=2] {'y'}, dimensions={0} | all-to-all | bytes 1048576 | tf_op jit(solution)/shard_map/front_sum/all_to_all | solution.py:273
  75.6 7.0 %collective-permute-start = (f32[64,256]{1,0:T(8,128)S(1)}, f32[64,256]{1,0:T(8,128)S(1)}, u32[]{:S(2)}, u32[]{:S(2)}) collective-permute-start(f32[64,256]{1,0:T(8,128)S(1)} %total.4), channel_id=1, source_target_pairs={{0,0},{1,16},{2,32},{3,48},{4,64},{5,80},{6,96},{7,112},{8,128},{9... | collective-permute-start | bytes 196616 | tf_op jit(solution)/shard_map/front_sum/ppermute | solution.py:309
  82.6 2.5 %collective-permute-done.piece_ref = f32[64,256]{1,0:T(8,128)S(1)} collective-permute-done((f32[64,256]{1,0:T(8,128)S(1)}, f32[64,256]{1,0:T(8,128)S(1)}, u32[]{:S(2)}, u32[]{:S(2)}) %collective-permute-start) | collective-permute-done | bytes 65568 | tf_op jit(solution)/shard_map/front_sum/ppermute | solution.py:309
  85.1 0.7 copy-done.4
  85.7 0.0 all-gather.3.cloned.1.call-update
  85.8 0.0 all-gather.5.cloned.1.call-done
  85.8 1.7 %copy-done.3 = f32[320,16,128]{2,1,0:T(8,128)S(1)} copy-done((f32[320,16,128]{2,1,0:T(8,128)S(1)}, f32[320,16,128]{2,1,0:T(8,128)}, u32[]{:S(2)}) %copy-start.3) | copy-done | bytes 2621464
  87.5 11.6 %factor_inverse.1.inverse_ref = f32[1024,1024]{1,0:T(8,128)S(1)} custom-call(f32[5120,128]{1,0:T(8,128)S(1)} %bitcast.20), custom_call_target="tpu_custom_call" | custom-call | tf_op jit(solution)/shard_map/inverse/factor_inverse/pallas_call | solution.py:151
  99.2 3.2 %separator.1 = f32[32,16,128]{2,1,0:T(8,128)S(1)} custom-call(s32[2]{0:T(128)S(1)} %pad_add_fusion.me_ref, s32[32]{0:T(128)S(1)} %copy-done.7, f32[64,256]{1,0:T(8,128)S(1)} %copy-done.5, f32[1,2,128,1024]{3,2,1,0:T(8,128)S(1)} %copy-done.2, f32[1024,1024]{1,0:T(8,128)S(1)} %factor_inverse.1.inverse_ref), custom_call_target="tpu_custom_call" | custom-call | tf_op jit(solution)/shard_map/separator/separator/pallas_call | solution.py:195
  102.4 24.0 %all_to_all.27.pieces_ref = f32[32,16,128]{2,1,0:T(8,128)S(1)} all-to-all(f32[32,16,128]{2,1,0:T(8,128)S(1)} %separator.1), channel_id=1, replica_groups=mesh['x'=4,'y'=8,'z'=8,'core'=2] {'x','y'}, dimensions={0} | all-to-all | bytes 524288 | tf_op jit(solution)/shard_map/separator/all_to_all | solution.py:273
  126.4 0.7 broadcast_in_dim.5
  127.1 9.4 %all-to-all-start.4 = ((f32[16,16,128]{2,1,0:T(8,128)}), f32[16,16,128]{2,1,0:T(8,128)S(1)}, u32[]{:S(2)}, u32[]{:S(2)}) async-start(f32[16,16,128]{2,1,0:T(8,128)} %broadcast_in_dim.5), calls=%async_computation.4 | async-start | bytes 262144 | tf_op jit(solution)/shard_map/separator/all_to_all | solution.py:273
  136.4 0.0 all-gather.3.cloned.1.call-done.whole_ref
  136.5 9.1 %all-to-all-done.4.blocks_ref = f32[16,16,128]{2,1,0:T(8,128)S(1)} async-done(((f32[16,16,128]{2,1,0:T(8,128)}), f32[16,16,128]{2,1,0:T(8,128)S(1)}, u32[]{:S(2)}, u32[]{:S(2)}) %all-to-all-start.4) | async-done | bytes 131104 | tf_op jit(solution)/shard_map/separator/all_to_all | solution.py:273
  145.6 6.5 %final.1 = (f32[1,2,128,1024]{3,2,1,0:T(8,128)}, f32[32,1024]{1,0:T(8,128)}) custom-call(s32[2]{0:T(128)S(1)} %pad_add_fusion.me_ref, s32[32]{0:T(128)S(1)} %copy-done.7, f32[1024,256]{1,0:T(8,128)} %all-gather.3.cloned.1.call-done.whole_ref, f32[16,16,128]{2,1,0:T(8,128)S(1)} %all-to-all-done.4.blocks_ref, f32[1024,1024]{1,0:T(8,128)} %copy-done.1), custom_call_target="tpu_custom_call" | custom-call | tf_op jit(solution)/shard_map/final/final/pallas_call | solution.py:229
  (19 shorter events, 0.2 us)
Async XLA Ops:
  7.2 0.9 copy-start
  8.9 20.2 %all-to-all-start = ((f32[32,2,1024]{2,1,0:T(2,128)}), f32[32,2,1024]{2,1,0:T(2,128)S(1)}, u32[]{:S(2)}, u32[]{:S(2)}) async-start(f32[32,2,1024]{2,1,0:T(2,128)} %broadcast_in_dim.4), calls=%async_computation | async-start | bytes 524288 | tf_op jit(solution)/shard_map/factor_gather/all_to_all | solution.py:273
  19.4 66.4 %all-gather.5.cloned.1.call-start = ((), (), s32[]{:S(2)}) async-start(), calls=%async_computation.6 | async-start | bytes 2785280 | tf_op jit(solution)/shard_map/factor_gather/all_gather | solution.py:284
  20.3 0.7 copy-start.6
  30.2 106.3 %all-gather.3.cloned.1.call-start = ((), (), s32[]{:S(2)}) async-start(), calls=%async_computation.5 | async-start | bytes 1114112 | tf_op jit(solution)/shard_map/front_gather/all_gather | solution.py:311
  75.6 9.5 %collective-permute-start = (f32[64,256]{1,0:T(8,128)S(1)}, f32[64,256]{1,0:T(8,128)S(1)}, u32[]{:S(2)}, u32[]{:S(2)}) collective-permute-start(f32[64,256]{1,0:T(8,128)S(1)} %total.4), channel_id=1, source_target_pairs={{0,0},{1,16},{2,32},{3,48},{4,64},{5,80},{6,96},{7,112},{8,128},{9... | collective-permute-start | bytes 196616 | tf_op jit(solution)/shard_map/front_sum/ppermute | solution.py:309
  85.1 0.7 copy-start.4
  85.8 1.7 %copy-start.3 = (f32[320,16,128]{2,1,0:T(8,128)S(1)}, f32[320,16,128]{2,1,0:T(8,128)}, u32[]{:S(2)}) copy-start(f32[320,16,128]{2,1,0:T(8,128)} %all-gather.5.cloned.1.call-done) | copy-start | bytes 7864324
  87.5 11.6 %copy-start.2 = (f32[1,2,128,1024]{3,2,1,0:T(8,128)S(1)}, f32[1,2,128,1024]{3,2,1,0:T(8,128)}, u32[]{:S(2)}) copy-start(f32[1,2,128,1024]{3,2,1,0:T(8,128)} %panel_ref.3) | copy-start | bytes 3145732
  87.5 11.6 %copy-start.5 = (f32[64,256]{1,0:T(8,128)S(1)}, f32[64,256]{1,0:T(8,128)}, u32[]{:S(2)}) copy-start(f32[64,256]{1,0:T(8,128)} %copy-done.4) | copy-start | bytes 196612
  87.5 11.6 %copy-start.7 = (s32[32]{0:T(128)S(1)}, s32[32]{0:T(128)}, u32[]{:S(2)}) copy-start(s32[32]{0:T(128)} %count_ref.5) | copy-start | bytes 388
  99.2 3.2 %copy-start.1 = (f32[1024,1024]{1,0:T(8,128)}, f32[1024,1024]{1,0:T(8,128)S(1)}, u32[]{:S(2)}) copy-start(f32[1024,1024]{1,0:T(8,128)S(1)} %factor_inverse.1.inverse_ref) | copy-start | bytes 12582916
  127.1 18.5 %all-to-all-start.4 = ((f32[16,16,128]{2,1,0:T(8,128)}), f32[16,16,128]{2,1,0:T(8,128)S(1)}, u32[]{:S(2)}, u32[]{:S(2)}) async-start(f32[16,16,128]{2,1,0:T(8,128)} %broadcast_in_dim.5), calls=%async_computation.4 | async-start | bytes 262144 | tf_op jit(solution)/shard_map/separator/all_to_all | solution.py:273
Sparse Core Ops, SparseCore 0:
  30.3 46.2 all-gather.4
  85.9 48.3 all-gather.2

commit v3 on v2

--- a/solution.py
+++ b/solution.py
@@ -10,16 +10,19 @@
 from jax.sharding import PartitionSpec as P
 
 ROW = ("x", "y")
-COL = ("z", "core")
-X, Y, Z, CORE = 4, 8, 8, 2
+COL = ("far", "near", "core")
+X, Y, FAR, NEAR, CORE = 4, 8, 4, 2, 2
+Z = FAR * NEAR
 N_ROW, N_COL = X * Y, Z * CORE
+SHARES = NEAR * CORE
+SWAP = [(0, 1), (1, 0)]
 TILE = 128
 SEP = 1024
 STRIPE = SEP // X
 PACKED = STRIPE * X * (X + 1) // 2
 WIDTH = SEP // N_COL
 OWN = SEP // N_ROW
-LINES = OWN // N_COL
+LINES = OWN // SHARES
 MIB = 1024 * 1024
 HIGHEST = lax.Precision.HIGHEST
 
@@ -100,17 +103,18 @@
     return inverses
 
 
-def inverse_kernel(share_ref, out_ref, packed_ref):
-    for block in range(PACKED // TILE):
+def inverse_kernel(me_ref, *refs):
+    share_refs, out_ref, packed_ref = refs[:SHARES], refs[SHARES], refs[SHARES + 1]
+    near, core = me_ref[2], me_ref[3]
+    for index, share_ref in enumerate(share_refs):
+        owner = lax.rem(near + index // CORE, NEAR) * CORE + lax.rem(core + index % CORE, CORE)
         for y in range(Y):
-            for line in range(LINES):
-                start = (block * Y + y) * LINES + line
-                taken = share_ref[pl.ds(start, N_COL, stride=PACKED // TILE * Y * LINES), :]
-                packed_ref[block, pl.ds(y * OWN + line, N_COL, stride=LINES), :] = taken
+            start = pl.multiple_of(y * OWN + owner * LINES, LINES)
+            packed_ref[pl.ds(start, LINES), :] = share_ref[y * LINES : (y + 1) * LINES, :]
 
     def factor(stripe, start, width):
-        first = (STRIPE * stripe * (stripe + 1) // 2 + start) // TILE
-        return jnp.concatenate([packed_ref[first + block] for block in range(width // TILE)], axis=1)
+        base = STRIPE * stripe * (stripe + 1) // 2
+        return packed_ref[:, base + start : base + start + width]
 
     diagonals = [factor(stripe, stripe * STRIPE, STRIPE) for stripe in range(X)]
     tiles = [d[p * TILE : (p + 1) * TILE, p * TILE : (p + 1) * TILE] for d in diagonals for p in range(2)]
@@ -147,16 +151,16 @@
 SMEM = pl.BlockSpec(memory_space=pltpu.SMEM)
 
 
-def factor_inverse(shares):
+def factor_inverse(me, shares):
     return pl.pallas_call(
         inverse_kernel,
-        in_specs=[VMEM],
+        in_specs=[SMEM] + [VMEM] * SHARES,
         out_specs=VMEM,
         out_shape=jax.ShapeDtypeStruct((SEP, SEP), jnp.float32),
-        scratch_shapes=[pltpu.VMEM((PACKED // TILE, STRIPE, TILE), jnp.float32)],
+        scratch_shapes=[pltpu.VMEM((STRIPE, PACKED), jnp.float32)],
         compiler_params=pltpu.CompilerParams(vmem_limit_bytes=20 * MIB),
         name="factor_inverse",
-    )(shares)
+    )(me, *shares)
 
 
 def times_inverse(left_ref, inverse_ref, stripe):
@@ -177,7 +181,8 @@
     row, col = me_ref[0], me_ref[1]
     live = [(slot < count_ref[row]).astype(jnp.float32) for slot in range(2)]
     strips = jnp.concatenate([panel_ref[0, slot] * live[slot] for slot in range(2)], axis=0)
-    local = exact_dot(piece_ref[...], strips)
+    piece = jnp.concatenate([piece_ref[:WIDTH], piece_ref[WIDTH:]], axis=1)
+    local = exact_dot(piece, strips)
     down = lax.broadcasted_iota(jnp.int32, (WIDTH, SEP), 0) + col * WIDTH
     across = lax.broadcasted_iota(jnp.int32, (WIDTH, SEP), 1)
     local = local + jnp.where((down == across) & (row == 0), 1.0, 0.0)
@@ -202,19 +207,20 @@
     )(me, slot_count, piece, panel, inverse)
 
 
-def final_kernel(me_ref, count_ref, whole_ref, blocks_ref, inverse_ref, update_ref, sep_ref, left_ref):
+def final_kernel(me_ref, count_ref, low_ref, high_ref, inverse_ref, update_ref, sep_ref, left_ref):
     @pl.when(pl.program_id(0) == 0)
     def _():
         row = me_ref[0]
-        turned = whole_ref[...].T
+        blocks = [ref[core, z] for ref in (low_ref, high_ref) for z in range(Z // 2) for core in range(CORE)]
         for slot in range(2):
             sign = -(slot < count_ref[row]).astype(jnp.float32)
-            left_ref[slot * TILE : (slot + 1) * TILE, :] = turned[slot * TILE : (slot + 1) * TILE] * sign
+            whole = jnp.concatenate([block[slot * WIDTH : (slot + 1) * WIDTH] for block in blocks], axis=0)
+            left_ref[slot * TILE : (slot + 1) * TILE, :] = whole.T * sign
         for side in range(2):
             lanes = slice(side * WIDTH, (side + 1) * WIDTH)
             start = 2 * TILE + side * (OWN // 2)
             left_ref[start : start + OWN // 2, :] = jnp.concatenate(
-                [blocks_ref[place][:, lanes] for place in range(N_COL)], axis=1
+                [block[2 * WIDTH :, lanes] for block in blocks], axis=1
             )
 
     @for_stripe
@@ -225,15 +231,15 @@
         sep_ref[...] = result[2 * TILE :]
 
 
-def final(me, slot_count, whole, blocks, inverse):
+def final(me, slot_count, low, high, inverse):
     return pl.pallas_call(
         final_kernel,
         grid=(X,),
         in_specs=[
             SMEM,
             SMEM,
-            whole_block((SEP, 2 * TILE)),
-            whole_block((N_COL, OWN // 2, 2 * WIDTH)),
+            whole_block(low.shape),
+            whole_block(high.shape),
             pl.BlockSpec((SEP, STRIPE), lambda i: (0, i)),
         ],
         out_specs=(
@@ -247,19 +253,26 @@
         scratch_shapes=[pltpu.VMEM((2 * TILE + OWN, SEP), jnp.float32)],
         compiler_params=pltpu.CompilerParams(vmem_limit_bytes=16 * MIB),
         name="final",
-    )(me, slot_count, off_chip(whole), blocks, off_chip(inverse))
+    )(me, slot_count, low, high, off_chip(inverse))
 
 
 def total_kernel(pieces_ref, out_ref):
-    out_ref[...] = jnp.sum(pieces_ref[...], axis=0)
-
-
-def total(pieces):
+    summed = jnp.sum(pieces_ref[...], axis=0)
+    rows = summed.shape[-2]
+    if summed.shape[-1] == out_ref.shape[-1]:
+        out_ref[...] = summed
+    else:
+        out_ref[:rows] = summed[:, :TILE]
+        out_ref[rows:] = summed[:, TILE:]
+
+
+def total(pieces, split=False):
+    shape = (2 * pieces.shape[1], TILE) if split else pieces.shape[1:]
     return pl.pallas_call(
         total_kernel,
         in_specs=[VMEM],
         out_specs=VMEM,
-        out_shape=jax.ShapeDtypeStruct(pieces.shape[1:], jnp.float32),
+        out_shape=jax.ShapeDtypeStruct(shape, jnp.float32),
         compiler_params=pltpu.CompilerParams(vmem_limit_bytes=8 * MIB),
         name="total",
     )(on_chip(pieces))
@@ -273,15 +286,19 @@
     return lax.all_to_all(blocks, axis, 0, 0, tiled=True)
 
 
-def spread_lines(sep_factor, col):
-    return exchange(spread(lax.dynamic_slice_in_dim(sep_factor, col * LINES, LINES, 0), N_ROW), ROW)
+def spread_lines(sep_factor, share):
+    return exchange(spread(lax.dynamic_slice_in_dim(sep_factor, share * LINES, LINES, 0), N_ROW), ROW)
 
 
 def gather_factor(lines):
-    stripes = lines.reshape(X, Y * LINES, SEP // TILE, TILE)
-    count = STRIPE // TILE
-    packed = jnp.concatenate([stripes[i, :, : count * (i + 1)].transpose(1, 0, 2) for i in range(X)], axis=0)
-    return lax.all_gather(packed, COL, axis=0, tiled=True).reshape(-1, TILE)
+    stripes = lines.reshape(X, Y * LINES, SEP)
+    packed = jnp.concatenate([stripes[i][:, : STRIPE * (i + 1)] for i in range(X)], axis=1)
+    return packed, lax.ppermute(packed, "core", SWAP), lax.ppermute(packed, "near", SWAP)
+
+
+def gather_blocks(block):
+    blocks = exchange(spread(block, Z), ("far", "near"))
+    return tuple(lax.all_gather(half, "core", axis=0) for half in (blocks[: Z // 2], blocks[Z // 2 :]))
 
 
 def to_slot_owner():
@@ -296,32 +313,37 @@
 def on_device(parent_sigma, slot_tile, slot_count, panel, sep_factor):
     my_row = lax.axis_index(ROW).astype(jnp.int32)
     my_col = lax.axis_index(COL).astype(jnp.int32)
-    me = jnp.stack([my_row, my_col])
+    near = lax.axis_index("near").astype(jnp.int32)
+    core = lax.axis_index("core").astype(jnp.int32)
+    me = jnp.stack([my_row, my_col, near, core])
     sigma = parent_sigma.reshape(4, TILE * 8, TILE)
     with jax.named_scope("front_product"):
-        partial = front(slot_tile, slot_count, me, sigma, panel).reshape(N_ROW, WIDTH, 2 * TILE)
+        partial = front(slot_tile, slot_count, me, sigma, panel).reshape(X, Y, WIDTH, 2 * TILE)
     with jax.named_scope("factor_gather"):
-        lines, partial = lax.optimization_barrier((spread_lines(sep_factor, my_col), partial))
+        lines, partial = lax.optimization_barrier((spread_lines(sep_factor, near * CORE + core), partial))
         shares = gather_factor(lines)
     with jax.named_scope("front_sum"):
-        half = total(exchange(partial.reshape(X, Y, WIDTH, 2 * TILE), "x"))
-        piece = total(exchange(half, "y"))
-        piece = lax.ppermute(piece, ROW + COL, to_slot_owner())
-    with jax.named_scope("front_gather"):
-        whole = lax.all_gather(piece, COL, axis=0, tiled=True)
+        pieces, near_share = lax.optimization_barrier((exchange(partial, "x"), shares[2]))
+        half = total(pieces)
+        shares = (*shares[:2], near_share, lax.ppermute(near_share, "core", SWAP))
+        pieces = exchange(half, "y")
     with jax.named_scope("inverse"):
-        shares, _ = lax.optimization_barrier((shares, piece))
-        inverse = factor_inverse(shares)
+        shares, _ = lax.optimization_barrier((shares, half))
+        inverse = factor_inverse(me, shares)
+    with jax.named_scope("front_place"):
+        pieces, inverse = lax.optimization_barrier((pieces, inverse))
+        piece = lax.ppermute(total(pieces, split=True), ROW + COL, to_slot_owner())
     with jax.named_scope("separator"):
         sent = separator(me, slot_count, piece, panel, inverse)
         taken = total(exchange(sent, ROW))
-        blocks = exchange(lax.optimization_barrier(spread(taken, N_COL)), COL)
+    with jax.named_scope("gather"):
+        low, high = gather_blocks(jnp.concatenate([piece, taken], axis=0))
     with jax.named_scope("final"):
-        return final(me, slot_count, whole, blocks, inverse)
+        return final(me, slot_count, low, high, inverse)
 
 
 def solution(mesh):
-    inner = Mesh(np.array(mesh.devices).reshape(X, Y, Z, CORE), ROW + COL)
+    inner = Mesh(np.array(mesh.devices).reshape(X, Y, FAR, NEAR, CORE), ROW + COL)
     placed = (
         P(None, ROW, None, None, COL, None),
         P(),

time: 159 us -> 174 us (1.094); the launches traced: 159 us -> 172 us
  waiting for transfers between devices: 15.5 us -> 39.6 us
  between operations: 14.2 us -> 0.86 us
  starting transfers between devices: 27 us -> 38.8 us
  blocking collectives: 69.3 us -> 59.5 us
    all_to_all x3 -> x2, blocking collectives: 69.3 us -> 49.7 us  [exchange(): return lax.all_to_all(blocks, axis, 0, 0, tiled=True)]
    all_to_all x2 -> x3, waiting for transfers between devices: 13 us -> 25.9 us  [exchange(): return lax.all_to_all(blocks, axis, 0, 0, tiled=True)]
    ppermute x1 -> x4, waiting for transfers between devices: 2.46 us -> 13.6 us  [the longest x1 10.1 us: gather_factor(): lax.ppermute(packed, 'near', SWAP)]
    all_gather x0 -> x2, blocking collectives: none -> 9.72 us  [gather_blocks(): lax.all_gather(half, 'core', axis=0)]
    ppermute x1 -> x4, starting transfers between devices: 7.02 us -> 14.2 us  [the longest x1 4.18 us: gather_factor(): lax.ppermute(packed, 'core', SWAP)]
    all_to_all x2 -> x3, starting transfers between devices: 19.9 us -> 24.6 us  [exchange(): return lax.all_to_all(blocks, axis, 0, 0, tiled=True)]
    unnamed x17 -> x15, local copies, waits for them, and re-layouts: 4.71 us -> 6.44 us
  transfers between devices with their start and end apart: 5 -> 7, of which waited for: 3 -> 5; matrix products, arithmetic and copies ran while one was open for 1% -> 0% of each run, Pallas kernels for 12% -> 9%
where the time goes in v3:
time: 174 us; the launch traced here: 172 us
  blocking collectives  59.5 us (34%)
  waiting for transfers between devices  39.6 us (23%)
  starting transfers between devices  38.8 us (22%)
  Pallas kernels  25.6 us (15%)
  local copies, waits for them, and re-layouts  7.73 us (4%)
    all_to_all x2, blocking collectives, exchange(): return lax.all_to_all(blocks, axis, 0, 0, tiled=True)  49.7 us
    all_to_all x3, waiting for transfers between devices, exchange(): return lax.all_to_all(blocks, axis, 0, 0, tiled=True)  25.9 us
    all_to_all x3, starting transfers between devices, exchange(): return lax.all_to_all(blocks, axis, 0, 0, tiled=True)  24.6 us
    pallas_call x1, Pallas kernels, factor_inverse(): pl.pallas_call(inverse_kernel, in_specs=[SMEM] + [VMEM] * SHARES, out_spe...  11.3 us
    ppermute x1, waiting for transfers between devices, gather_factor(): lax.ppermute(packed, 'near', SWAP)  10.1 us
    all_gather x2, blocking collectives, gather_blocks(): lax.all_gather(half, 'core', axis=0)  9.72 us
    unnamed x15, local copies, waits for them, and re-layouts  6.44 us
    pallas_call x1, Pallas kernels, final(): pl.pallas_call(final_kernel, grid=(X,), in_specs=[SMEM, SMEM, whole_block...  6.13 us
  transfers between devices with their start and end apart: 7, of which 5 were waited for; matrix products, arithmetic and copies ran while one was open for 0% of the time, Pallas kernels for 9%

profile of v3, /device:TPU:1, one launch (start us, length us, event | category | flops | bytes accessed | tf_op | source)
XLA Modules:
  0.0 172.0 jit_solution(13740491811004640887)
XLA Ops:
  0.6 0.0 copy-start
  0.7 0.9 copy-done
  1.5 1.1 broadcast_in_dim.4
  2.6 10.5 %all-to-all-start = ((f32[32,8,1024]{2,1,0:T(8,128)}), f32[32,8,1024]{2,1,0:T(8,128)S(1)}, u32[]{:S(2)}, u32[]{:S(2)}) async-start(f32[32,8,1024]{2,1,0:T(8,128)} %broadcast_in_dim.4), calls=%async_computation | async-start | bytes 2097152 | tf_op jit(solution)/shard_map/factor_gather/all_to_all | solution.py:286
  13.2 0.1 copy.8.tile_ref
  13.3 0.1 pad_add_fusion.me_ref
  13.3 4.3 %front.1 = f32[2,1024,256]{2,1,0:T(8,128)S(1)} custom-call(s32[32,2]{1,0:T(8,128)S(1)} %copy.8.tile_ref, s32[32]{0:T(128)S(1)} %copy-done.5, s32[4]{0:T(128)S(1)} %pad_add_fusion.me_ref, f32[4,1024,128]{2,1,0:T(8,128)} %bitcast.19, f32[4,1024,128]{2,1,0:T(8,128)} %bitcast.20, f32[1,2,128,1024]{3,2,1,0:T(8,128)} %panel_ref.3), custom_call_target="tpu_custom_call" | custom-call | tf_op jit(solution)/shard_map/front_product/front/pallas_call | solution.py:66
  17.6 1.3 copy-done.3
  19.0 18.8 %all-to-all-done = f32[32,8,1024]{2,1,0:T(8,128)S(1)} async-done(((f32[32,8,1024]{2,1,0:T(8,128)}), f32[32,8,1024]{2,1,0:T(8,128)S(1)}, u32[]{:S(2)}, u32[]{:S(2)}) %all-to-all-start) | async-done | bytes 1048608 | tf_op jit(solution)/shard_map/factor_gather/all_to_all | solution.py:286
  37.8 3.6 %all-to-all-start.1 = ((f32[4,8,64,256]{3,2,1,0:T(8,128)}), f32[4,8,64,256]{3,2,1,0:T(8,128)S(1)}, u32[]{:S(2)}, u32[]{:S(2)}) async-start(f32[4,8,64,256]{3,2,1,0:T(8,128)} %bitcast.16), calls=%async_computation.1 | async-start | bytes 4194304 | tf_op jit(solution)/shard_map/front_sum/all_to_all | solution.py:286
  41.4 0.1 slice_bitcast_fusion.3
  41.6 4.0 %collective-permute-start = (f32[64,2560]{1,0:T(8,128)S(1)}, f32[64,2560]{1,0:T(8,128)S(1)}, u32[]{:S(2)}, u32[]{:S(2)}) collective-permute-start(f32[64,2560]{1,0:T(8,128)S(1)} %pad_maximum_fusion.refs_0_), channel_id=1, source_target_pairs={{0,2},{2,0},{1,3},{3,1},{4,6},{6,4},{5,7},{7,5},{8,10},{10,8},{9,1... | collective-permute-start | bytes 1966088 | tf_op jit(solution)/shard_map/factor_gather/ppermute | solution.py:296
  45.6 10.1 %collective-permute-done.refs_2_ = f32[64,2560]{1,0:T(8,128)S(1)} collective-permute-done((f32[64,2560]{1,0:T(8,128)S(1)}, f32[64,2560]{1,0:T(8,128)S(1)}, u32[]{:S(2)}, u32[]{:S(2)}) %collective-permute-start) | collective-permute-done | bytes 655392 | tf_op jit(solution)/shard_map/factor_gather/ppermute | solution.py:296
  55.7 7.1 %all-to-all-done.1.pieces_ref = f32[4,8,64,256]{3,2,1,0:T(8,128)S(1)} async-done(((f32[4,8,64,256]{3,2,1,0:T(8,128)}), f32[4,8,64,256]{3,2,1,0:T(8,128)S(1)}, u32[]{:S(2)}, u32[]{:S(2)}) %all-to-all-start.1) | async-done | bytes 2097184 | tf_op jit(solution)/shard_map/front_sum/all_to_all | solution.py:286
  62.7 0.9 total.3
  63.6 10.5 %all-to-all-start.2 = ((f32[8,64,256]{2,1,0:T(8,128)}), f32[8,64,256]{2,1,0:T(8,128)S(1)}, u32[]{:S(2)}, u32[]{:S(2)}) async-start(f32[8,64,256]{2,1,0:T(8,128)} %total.3), calls=%async_computation.2 | async-start | bytes 1048576 | tf_op jit(solution)/shard_map/front_sum/all_to_all | solution.py:286
  74.1 4.2 %collective-permute-start.1 = (f32[64,2560]{1,0:T(8,128)S(1)}, f32[64,2560]{1,0:T(8,128)S(1)}, u32[]{:S(2)}, u32[]{:S(2)}) collective-permute-start(f32[64,2560]{1,0:T(8,128)S(1)} %pad_maximum_fusion.refs_0_), channel_id=1, source_target_pairs={{0,1},{1,0},{2,3},{3,2},{4,5},{5,4},{6,7},{7,6},{8,9},{9,8},{10,11... | collective-permute-start | bytes 1966088 | tf_op jit(solution)/shard_map/factor_gather/ppermute | solution.py:296
  78.3 2.1 %collective-permute-start.2 = (f32[64,2560]{1,0:T(8,128)S(1)}, f32[64,2560]{1,0:T(8,128)S(1)}, u32[]{:S(2)}, u32[]{:S(2)}) collective-permute-start(f32[64,2560]{1,0:T(8,128)S(1)} %collective-permute-done.refs_2_), channel_id=1, source_target_pairs={{0,1},{1,0},{2,3},{3,2},{4,5},{5,4},{6,7},{7,6},{8,9},{9,8},{10,11... | collective-permute-start | bytes 1966088 | tf_op jit(solution)/shard_map/front_sum/ppermute | solution.py:328
  80.4 0.0 collective-permute-done.1.refs_1_
  80.4 1.9 %collective-permute-done.2.refs_3_ = f32[64,2560]{1,0:T(8,128)S(1)} collective-permute-done((f32[64,2560]{1,0:T(8,128)S(1)}, f32[64,2560]{1,0:T(8,128)S(1)}, u32[]{:S(2)}, u32[]{:S(2)}) %collective-permute-start.2) | collective-permute-done | bytes 655392 | tf_op jit(solution)/shard_map/front_sum/ppermute | solution.py:328
  82.3 11.3 %factor_inverse.1.inverse_ref = f32[1024,1024]{1,0:T(8,128)S(1)} custom-call(s32[4]{0:T(128)S(1)} %pad_add_fusion.me_ref, f32[64,2560]{1,0:T(8,128)S(1)} %pad_maximum_fusion.refs_0_, f32[64,2560]{1,0:T(8,128)S(1)} %collective-permute-done.1.refs_1_, f32[64,2560]{1,0:T(8,128)S(1)} %collective-permute-done.refs_2_, f32[64,2560]{1,0:T(8,128)S(1)} %collective-permute-done.2.refs_3_), custom_call_target="tpu_custom_call" | custom-call | tf_op jit(solution)/shard_map/inverse/factor_inverse/pallas_call | solution.py:155
  93.6 1.9 %copy-done.1 = f32[1024,1024]{1,0:T(8,128)} copy-done((f32[1024,1024]{1,0:T(8,128)}, f32[1024,1024]{1,0:T(8,128)S(1)}, u32[]{:S(2)}) %copy-start.1) | copy-done | bytes 4194328
  95.5 0.0 all-to-all-done.2.pieces_ref
  95.6 3.9 %collective-permute-start.3 = (f32[128,128]{1,0:T(8,128)S(1)}, f32[128,128]{1,0:T(8,128)S(1)}, u32[]{:S(2)}, u32[]{:S(2)}) collective-permute-start(f32[128,128]{1,0:T(8,128)S(1)} %total.4), channel_id=1, source_target_pairs={{0,0},{1,16},{2,32},{3,48},{4,64},{5,80},{6,96},{7,112},{8,128},{9... | collective-permute-start | bytes 196616 | tf_op jit(solution)/shard_map/front_place/ppermute | solution.py:335
  99.5 1.7 collective-permute-done.3.piece_ref
  101.2 2.2 %copy-done.2 = f32[1024,1024]{1,0:T(8,128)S(1)} copy-done((f32[1024,1024]{1,0:T(8,128)S(1)}, f32[1024,1024]{1,0:T(8,128)}, u32[]{:S(2)}) %copy-start.2) | copy-done | bytes 4194328
  103.4 2.9 %separator.1 = f32[32,16,128]{2,1,0:T(8,128)S(1)} custom-call(s32[4]{0:T(128)S(1)} %pad_add_fusion.me_ref, s32[32]{0:T(128)S(1)} %copy-done.5, f32[128,128]{1,0:T(8,128)S(1)} %collective-permute-done.3.piece_ref, f32[1,2,128,1024]{3,2,1,0:T(8,128)S(1)} %copy-done.4, f32[1024,1024]{1,0:T(8,128)S(1)} %copy-done.2), custom_call_target="tpu_custom_call" | custom-call | tf_op jit(solution)/shard_map/separator/separator/pallas_call | solution.py:200
  106.3 26.2 %all_to_all.25.pieces_ref = f32[32,16,128]{2,1,0:T(8,128)S(1)} all-to-all(f32[32,16,128]{2,1,0:T(8,128)S(1)} %separator.1), channel_id=1, replica_groups=mesh['x'=4,'y'=8,'far'=4,'near'=2,'core'=2] {'x','y'}, dimensions={0} | all-to-all | bytes 524288 | tf_op jit(solution)/shard_map/separator/all_to_all | solution.py:286
  132.7 23.5 %all_to_all.26 = f32[8,144,128]{2,1,0:T(8,128)S(1)} all-to-all(f32[8,144,128]{2,1,0:T(8,128)S(1)} %broadcast_in_dim.5), channel_id=1, replica_groups=mesh['x'=4,'y'=8,'far'=4,'near'=2,'core'=2] {'far','near'}, dimensions={0} | all-to-all | bytes 1179648 | tf_op jit(solution)/shard_map/gather/all_to_all | solution.py:286
  156.2 7.5 %all-gather.1 = f32[8,144,128]{2,1,0:T(8,128)S(1)} all-gather(f32[4,144,128]{2,1,0:T(8,128)S(1)} %get-tuple-element.26), channel_id=3, replica_groups=mesh['x'=4,'y'=8,'far'=4,'near'=2,'core'=2] {'core'}, dimensions={0}, use_global_device_ids=true | all-gather | bytes 884736 | tf_op jit(solution)/shard_map/gather/all_gather | solution.py:301
  163.7 2.2 %all-gather = f32[8,144,128]{2,1,0:T(8,128)S(1)} all-gather(f32[4,144,128]{2,1,0:T(8,128)S(1)} %get-tuple-element.27), channel_id=2, replica_groups=mesh['x'=4,'y'=8,'far'=4,'near'=2,'core'=2] {'core'}, dimensions={0}, use_global_device_ids=true | all-gather | bytes 884736 | tf_op jit(solution)/shard_map/gather/all_gather | solution.py:301
  165.9 6.1 %final.1 = (f32[1,2,128,1024]{3,2,1,0:T(8,128)}, f32[32,1024]{1,0:T(8,128)}) custom-call(s32[4]{0:T(128)S(1)} %pad_add_fusion.me_ref, s32[32]{0:T(128)S(1)} %copy-done.5, f32[2,4,144,128]{3,2,1,0:T(8,128)S(1)} %bitcast.18, f32[2,4,144,128]{3,2,1,0:T(8,128)S(1)} %bitcast.17, f32[1024,1024]{1,0:T(8,128)} %copy-done.1), custom_call_target="tpu_custom_call" | custom-call | tf_op jit(solution)/shard_map/final/final/pallas_call | solution.py:235
  (19 shorter events, 0.3 us)
Async XLA Ops:
  0.6 0.9 copy-start
  0.6 12.5 %copy-start.6 = (s32[32,2]{0,1:T(2,128)S(1)}, s32[32,2]{0,1:T(2,128)}, u32[]{:S(2)}) copy-start(s32[32,2]{0,1:T(2,128)} %param.6) | copy-start | bytes 772
  0.7 12.7 %copy-start.5 = (s32[32]{0:T(128)S(1)}, s32[32]{0:T(128)}, u32[]{:S(2)}) copy-start(s32[32]{0:T(128)} %count_ref.5) | copy-start | bytes 388
  2.6 35.1 %all-to-all-start = ((f32[32,8,1024]{2,1,0:T(8,128)}), f32[32,8,1024]{2,1,0:T(8,128)S(1)}, u32[]{:S(2)}, u32[]{:S(2)}) async-start(f32[32,8,1024]{2,1,0:T(8,128)} %broadcast_in_dim.4), calls=%async_computation | async-start | bytes 2097152 | tf_op jit(solution)/shard_map/factor_gather/all_to_all | solution.py:286
  17.6 1.3 copy-start.3
  37.8 25.0 %all-to-all-start.1 = ((f32[4,8,64,256]{3,2,1,0:T(8,128)}), f32[4,8,64,256]{3,2,1,0:T(8,128)S(1)}, u32[]{:S(2)}, u32[]{:S(2)}) async-start(f32[4,8,64,256]{3,2,1,0:T(8,128)} %bitcast.16), calls=%async_computation.1 | async-start | bytes 4194304 | tf_op jit(solution)/shard_map/front_sum/all_to_all | solution.py:286
  41.6 14.1 %collective-permute-start = (f32[64,2560]{1,0:T(8,128)S(1)}, f32[64,2560]{1,0:T(8,128)S(1)}, u32[]{:S(2)}, u32[]{:S(2)}) collective-permute-start(f32[64,2560]{1,0:T(8,128)S(1)} %pad_maximum_fusion.refs_0_), channel_id=1, source_target_pairs={{0,2},{2,0},{1,3},{3,1},{4,6},{6,4},{5,7},{7,5},{8,10},{10,8},{9,1... | collective-permute-start | bytes 1966088 | tf_op jit(solution)/shard_map/factor_gather/ppermute | solution.py:296
  63.6 31.9 %all-to-all-start.2 = ((f32[8,64,256]{2,1,0:T(8,128)}), f32[8,64,256]{2,1,0:T(8,128)S(1)}, u32[]{:S(2)}, u32[]{:S(2)}) async-start(f32[8,64,256]{2,1,0:T(8,128)} %total.3), calls=%async_computation.2 | async-start | bytes 1048576 | tf_op jit(solution)/shard_map/front_sum/all_to_all | solution.py:286
  74.1 27.1 %copy-start.4 = (f32[1,2,128,1024]{3,2,1,0:T(8,128)S(1)}, f32[1,2,128,1024]{3,2,1,0:T(8,128)}, u32[]{:S(2)}) copy-start(f32[1,2,128,1024]{3,2,1,0:T(8,128)} %panel_ref.3) | copy-start | bytes 3145732
  74.1 6.3 %collective-permute-start.1 = (f32[64,2560]{1,0:T(8,128)S(1)}, f32[64,2560]{1,0:T(8,128)S(1)}, u32[]{:S(2)}, u32[]{:S(2)}) collective-permute-start(f32[64,2560]{1,0:T(8,128)S(1)} %pad_maximum_fusion.refs_0_), channel_id=1, source_target_pairs={{0,1},{1,0},{2,3},{3,2},{4,5},{5,4},{6,7},{7,6},{8,9},{9,8},{10,11... | collective-permute-start | bytes 1966088 | tf_op jit(solution)/shard_map/factor_gather/ppermute | solution.py:296
  78.3 4.0 %collective-permute-start.2 = (f32[64,2560]{1,0:T(8,128)S(1)}, f32[64,2560]{1,0:T(8,128)S(1)}, u32[]{:S(2)}, u32[]{:S(2)}) collective-permute-start(f32[64,2560]{1,0:T(8,128)S(1)} %collective-permute-done.refs_2_), channel_id=1, source_target_pairs={{0,1},{1,0},{2,3},{3,2},{4,5},{5,4},{6,7},{7,6},{8,9},{9,8},{10,11... | collective-permute-start | bytes 1966088 | tf_op jit(solution)/shard_map/front_sum/ppermute | solution.py:328
  93.6 2.0 %copy-start.1 = (f32[1024,1024]{1,0:T(8,128)}, f32[1024,1024]{1,0:T(8,128)S(1)}, u32[]{:S(2)}) copy-start(f32[1024,1024]{1,0:T(8,128)S(1)} %factor_inverse.1.inverse_ref) | copy-start | bytes 12582916
  95.6 5.6 %collective-permute-start.3 = (f32[128,128]{1,0:T(8,128)S(1)}, f32[128,128]{1,0:T(8,128)S(1)}, u32[]{:S(2)}, u32[]{:S(2)}) collective-permute-start(f32[128,128]{1,0:T(8,128)S(1)} %total.4), channel_id=1, source_target_pairs={{0,0},{1,16},{2,32},{3,48},{4,64},{5,80},{6,96},{7,112},{8,128},{9... | collective-permute-start | bytes 196616 | tf_op jit(solution)/shard_map/front_place/ppermute | solution.py:335
  101.2 2.2 %copy-start.2 = (f32[1024,1024]{1,0:T(8,128)S(1)}, f32[1024,1024]{1,0:T(8,128)}, u32[]{:S(2)}) copy-start(f32[1024,1024]{1,0:T(8,128)} %copy-done.1) | copy-start | bytes 12582916

commit v4 on v2

--- a/solution.py
+++ b/solution.py
@@ -21,11 +21,23 @@
 OWN = SEP // N_ROW
 LINES = OWN // N_COL
 MIB = 1024 * 1024
-HIGHEST = lax.Precision.HIGHEST
-
-
-def exact_dot(left, right):
-    return jnp.dot(left, right, precision=HIGHEST, preferred_element_type=jnp.float32)
+
+
+def split(value):
+    high = value.astype(jnp.bfloat16)
+    return high, (value - high.astype(jnp.float32)).astype(jnp.bfloat16)
+
+
+def split_dot(left, right):
+    def dot(first, last):
+        return jnp.dot(first, last, preferred_element_type=jnp.float32)
+
+    (left_high, left_low), (right_high, right_low) = left, right
+    return dot(left_high, right_high) + (dot(left_high, right_low) + dot(left_low, right_high))
+
+
+def fine_dot(left, right):
+    return split_dot(split(left), split(right))
 
 
 def on_chip(value):
@@ -53,7 +65,7 @@
             ],
             axis=0,
         )
-        out_ref[step] = exact_dot(strips_t, block)
+        out_ref[step] = fine_dot(strips_t, block)
 
 
 def front(slot_tile, slot_count, me, sigma, panel):
@@ -94,8 +106,11 @@
     size = 2
     while size < TILE:
         mask = left_of(size)
-        products = [exact_dot(jnp.where(mask, tile, 0.0), inverse) for tile, inverse in zip(tiles, inverses)]
-        inverses = [inverse - exact_dot(inverse, product) for inverse, product in zip(inverses, products)]
+        halves = [split(inverse) for inverse in inverses]
+        products = [split_dot(split(jnp.where(mask, tile, 0.0)), half) for tile, half in zip(tiles, halves)]
+        inverses = [
+            inverse - split_dot(half, split(product)) for inverse, half, product in zip(inverses, halves, products)
+        ]
         size *= 2
     return inverses
 
@@ -115,8 +130,8 @@
     diagonals = [factor(stripe, stripe * STRIPE, STRIPE) for stripe in range(X)]
     tiles = [d[p * TILE : (p + 1) * TILE, p * TILE : (p + 1) * TILE] for d in diagonals for p in range(2)]
     inverses = invert_tiles(tiles)
-    middles = [exact_dot(d[TILE:, :TILE], inverses[2 * stripe]) for stripe, d in enumerate(diagonals)]
-    corners = [-exact_dot(inverses[2 * stripe + 1], middle) for stripe, middle in enumerate(middles)]
+    middles = [fine_dot(d[TILE:, :TILE], inverses[2 * stripe]) for stripe, d in enumerate(diagonals)]
+    corners = [-fine_dot(inverses[2 * stripe + 1], middle) for stripe, middle in enumerate(middles)]
     for stripe in range(X):
         top = stripe * STRIPE
         out_ref[top : top + TILE, top : top + TILE] = inverses[2 * stripe]
@@ -129,18 +144,18 @@
     for stripe in (1, 3):
         left = (stripe - 1) * STRIPE
         above = out_ref[left : left + STRIPE, left : left + STRIPE]
-        products.append(exact_dot(factor(stripe, left, STRIPE), above))
+        products.append(fine_dot(factor(stripe, left, STRIPE), above))
     for stripe, product in zip((1, 3), products):
         top = stripe * STRIPE
         own = out_ref[top : top + STRIPE, top : top + STRIPE]
-        out_ref[top : top + STRIPE, top - STRIPE : top] = -exact_dot(own, product)
+        out_ref[top : top + STRIPE, top - STRIPE : top] = -fine_dot(own, product)
     half = 2 * STRIPE
     left_part = jnp.concatenate([factor(2, 0, half), factor(3, 0, half)], axis=0)
-    first_cols = exact_dot(left_part, out_ref[:half, :STRIPE])
-    last_cols = exact_dot(left_part[:, STRIPE:], out_ref[STRIPE:half, STRIPE:half])
+    first_cols = fine_dot(left_part, out_ref[:half, :STRIPE])
+    last_cols = fine_dot(left_part[:, STRIPE:], out_ref[STRIPE:half, STRIPE:half])
     product = jnp.concatenate([first_cols, last_cols], axis=1)
-    out_ref[half : half + STRIPE, :half] = -exact_dot(out_ref[half : half + STRIPE, half : half + STRIPE], product[:STRIPE])
-    out_ref[half + STRIPE :, :half] = -exact_dot(out_ref[half + STRIPE :, half:], product)
+    out_ref[half : half + STRIPE, :half] = -fine_dot(out_ref[half : half + STRIPE, half : half + STRIPE], product[:STRIPE])
+    out_ref[half + STRIPE :, :half] = -fine_dot(out_ref[half + STRIPE :, half:], product)
 
 
 VMEM = pl.BlockSpec(memory_space=pltpu.VMEM)
@@ -161,7 +176,7 @@
 
 def times_inverse(left_ref, inverse_ref, stripe):
     start = stripe * STRIPE
-    return exact_dot(left_ref[:, start:], inverse_ref[start:, :])
+    return fine_dot(left_ref[:, start:], inverse_ref[start:, :])
 
 
 def for_stripe(body):
@@ -177,13 +192,13 @@
     row, col = me_ref[0], me_ref[1]
     live = [(slot < count_ref[row]).astype(jnp.float32) for slot in range(2)]
     strips = jnp.concatenate([panel_ref[0, slot] * live[slot] for slot in range(2)], axis=0)
-    local = exact_dot(piece_ref[...], strips)
+    local = fine_dot(piece_ref[...], strips)
     down = lax.broadcasted_iota(jnp.int32, (WIDTH, SEP), 0) + col * WIDTH
     across = lax.broadcasted_iota(jnp.int32, (WIDTH, SEP), 1)
     local = local + jnp.where((down == across) & (row == 0), 1.0, 0.0)
     for stripe in range(X):
         first = stripe * STRIPE
-        turned = exact_dot(local[:, first:], inverse_ref[first:, first : first + STRIPE]).T
+        turned = fine_dot(local[:, first:], inverse_ref[first:, first : first + STRIPE]).T
         for place in range(STRIPE // OWN):
             start = place * OWN
             out_ref[stripe * (STRIPE // OWN) + place] = jnp.concatenate(

time: 159 us -> 152 us (0.956)
  Pallas kernels: 25.7 us -> 17.7 us
    pallas_call x1, Pallas kernels: 11.6 us -> 6.64 us  [factor_inverse(): pl.pallas_call(inverse_kernel, in_specs=[VMEM], out_specs=VMEM, out_shape...]
    all_gather x1, waiting for transfers between devices: 0.01 us -> 4.03 us  [on_device(): whole = lax.all_gather(piece, COL, axis=0, tiled=True)]
    all_to_all x2, waiting for transfers between devices: 13 us -> 9.82 us  [exchange(): return lax.all_to_all(blocks, axis, 0, 0, tiled=True)]
  transfers between devices with their start and end apart: 5 -> 5, of which waited for: 3 -> 4; matrix products, arithmetic and copies ran while one was open for 1% -> 1% of each run, Pallas kernels for 12% -> 8%
where the time goes in v4:
time: 152 us
  blocking collectives  69.3 us (46%)
  starting transfers between devices  26.8 us (18%)
  Pallas kernels  17.7 us (12%)
  waiting for transfers between devices  16.5 us (11%)
  between operations  14.2 us (9%)
  local copies, waits for them, and re-layouts  7.14 us (5%)
    all_to_all x3, blocking collectives, exchange(): return lax.all_to_all(blocks, axis, 0, 0, tiled=True)  69.3 us
    all_to_all x2, starting transfers between devices, exchange(): return lax.all_to_all(blocks, axis, 0, 0, tiled=True)  19.9 us
    all_to_all x2, waiting for transfers between devices, exchange(): return lax.all_to_all(blocks, axis, 0, 0, tiled=True)  9.82 us
    ppermute x1, starting transfers between devices, on_device(): piece = lax.ppermute(piece, ROW + COL, to_slot_owner())  6.84 us
    pallas_call x1, Pallas kernels, factor_inverse(): pl.pallas_call(inverse_kernel, in_specs=[VMEM], out_specs=VMEM, out_shape...  6.64 us
    pallas_call x1, Pallas kernels, final(): pl.pallas_call(final_kernel, grid=(X,), in_specs=[SMEM, SMEM, whole_block...  5.47 us
    unnamed x17, local copies, waits for them, and re-layouts  4.71 us
    all_gather x1, waiting for transfers between devices, on_device(): whole = lax.all_gather(piece, COL, axis=0, tiled=True)  4.03 us
  transfers between devices with their start and end apart: 5, of which 4 were waited for; matrix products, arithmetic and copies ran while one was open for 1% of the time, Pallas kernels for 8%

profile of v4, /device:TPU:1, one launch (start us, length us, event | category | flops | bytes accessed | tf_op | source)
XLA Modules:
  0.0 151.7 jit_solution(8006365499713256464)
XLA Ops:
  7.2 0.0 copy-start
  7.2 0.9 copy-done
  8.1 0.8 broadcast_in_dim.4
  8.9 10.5 %all-to-all-start = ((f32[32,2,1024]{2,1,0:T(2,128)}), f32[32,2,1024]{2,1,0:T(2,128)S(1)}, u32[]{:S(2)}, u32[]{:S(2)}) async-start(f32[32,2,1024]{2,1,0:T(2,128)} %broadcast_in_dim.4), calls=%async_computation | async-start | bytes 524288 | tf_op jit(solution)/shard_map/factor_gather/all_to_all | solution.py:288
  19.4 0.0 all-gather.5.cloned.1.call-start
  19.4 0.8 copy.10.tile_ref
  20.2 0.1 pad_add_fusion.me_ref
  20.3 0.7 copy-done.6
  20.9 3.5 %front.1 = f32[2,1024,256]{2,1,0:T(8,128)S(1)} custom-call(s32[32,2]{1,0:T(8,128)S(1)} %copy.10.tile_ref, s32[32]{0:T(128)S(1)} %copy-done.6, s32[2]{0:T(128)S(1)} %pad_add_fusion.me_ref, f32[4,1024,128]{2,1,0:T(8,128)} %bitcast.21, f32[4,1024,128]{2,1,0:T(8,128)} %bitcast.22, f32[1,2,128,1024]{3,2,1,0:T(8,128)} %panel_ref.3), custom_call_target="tpu_custom_call" | custom-call | tf_op jit(solution)/shard_map/front_product/front/pallas_call | solution.py:75
  24.4 4.7 %all-to-all-done = f32[32,2,1024]{2,1,0:T(2,128)S(1)} async-done(((f32[32,2,1024]{2,1,0:T(2,128)}), f32[32,2,1024]{2,1,0:T(2,128)S(1)}, u32[]{:S(2)}, u32[]{:S(2)}) %all-to-all-start) | async-done | bytes 262176 | tf_op jit(solution)/shard_map/factor_gather/all_to_all | solution.py:288
  29.1 0.2 reshape.26
  29.3 0.1 squeeze.15
  29.4 0.7 copy.11
  30.1 0.0 all-gather.5.cloned.1.call-update
  30.2 0.0 all-gather.3.cloned.1.call-start
  30.2 25.1 %all_to_all.25.pieces_ref = f32[4,8,64,256]{3,2,1,0:T(8,128)S(1)} all-to-all(f32[4,8,64,256]{3,2,1,0:T(8,128)S(1)} %bitcast.19), channel_id=1, replica_groups=mesh['x'=4,'y'=8,'z'=8,'core'=2] {'x'}, dimensions={0} | all-to-all | bytes 4194304 | tf_op jit(solution)/shard_map/front_sum/all_to_all | solution.py:288
  55.3 0.1 total.3
  55.4 20.2 %all_to_all.26.pieces_ref = f32[8,64,256]{2,1,0:T(8,128)S(1)} all-to-all(f32[8,64,256]{2,1,0:T(8,128)S(1)} %total.3), channel_id=1, replica_groups=mesh['x'=4,'y'=8,'z'=8,'core'=2] {'y'}, dimensions={0} | all-to-all | bytes 1048576 | tf_op jit(solution)/shard_map/front_sum/all_to_all | solution.py:288
  75.6 6.8 %collective-permute-start = (f32[64,256]{1,0:T(8,128)S(1)}, f32[64,256]{1,0:T(8,128)S(1)}, u32[]{:S(2)}, u32[]{:S(2)}) collective-permute-start(f32[64,256]{1,0:T(8,128)S(1)} %total.4), channel_id=1, source_target_pairs={{0,0},{1,16},{2,32},{3,48},{4,64},{5,80},{6,96},{7,112},{8,128},{9... | collective-permute-start | bytes 196616 | tf_op jit(solution)/shard_map/front_sum/ppermute | solution.py:324
  82.5 2.6 %collective-permute-done.piece_ref = f32[64,256]{1,0:T(8,128)S(1)} collective-permute-done((f32[64,256]{1,0:T(8,128)S(1)}, f32[64,256]{1,0:T(8,128)S(1)}, u32[]{:S(2)}, u32[]{:S(2)}) %collective-permute-start) | collective-permute-done | bytes 65568 | tf_op jit(solution)/shard_map/front_sum/ppermute | solution.py:324
  85.1 0.7 copy-done.4
  85.7 0.0 all-gather.3.cloned.1.call-update
  85.8 0.0 all-gather.5.cloned.1.call-done
  85.8 1.7 %copy-done.3 = f32[320,16,128]{2,1,0:T(8,128)S(1)} copy-done((f32[320,16,128]{2,1,0:T(8,128)S(1)}, f32[320,16,128]{2,1,0:T(8,128)}, u32[]{:S(2)}) %copy-start.3) | copy-done | bytes 2621464
  87.5 6.6 %factor_inverse.1.inverse_ref = f32[1024,1024]{1,0:T(8,128)S(1)} custom-call(f32[5120,128]{1,0:T(8,128)S(1)} %bitcast.20), custom_call_target="tpu_custom_call" | custom-call | tf_op jit(solution)/shard_map/inverse/factor_inverse/pallas_call | solution.py:166
  94.2 1.9 %separator.1 = f32[32,16,128]{2,1,0:T(8,128)S(1)} custom-call(s32[2]{0:T(128)S(1)} %pad_add_fusion.me_ref, s32[32]{0:T(128)S(1)} %copy-done.7, f32[64,256]{1,0:T(8,128)S(1)} %copy-done.5, f32[1,2,128,1024]{3,2,1,0:T(8,128)S(1)} %copy-done.2, f32[1024,1024]{1,0:T(8,128)S(1)} %factor_inverse.1.inverse_ref), custom_call_target="tpu_custom_call" | custom-call | tf_op jit(solution)/shard_map/separator/separator/pallas_call | solution.py:210
  96.2 24.0 %all_to_all.27.pieces_ref = f32[32,16,128]{2,1,0:T(8,128)S(1)} all-to-all(f32[32,16,128]{2,1,0:T(8,128)S(1)} %separator.1), channel_id=1, replica_groups=mesh['x'=4,'y'=8,'z'=8,'core'=2] {'x','y'}, dimensions={0} | all-to-all | bytes 524288 | tf_op jit(solution)/shard_map/separator/all_to_all | solution.py:288
  120.2 0.7 broadcast_in_dim.5
  120.9 9.4 %all-to-all-start.4 = ((f32[16,16,128]{2,1,0:T(8,128)}), f32[16,16,128]{2,1,0:T(8,128)S(1)}, u32[]{:S(2)}, u32[]{:S(2)}) async-start(f32[16,16,128]{2,1,0:T(8,128)} %broadcast_in_dim.5), calls=%async_computation.4 | async-start | bytes 262144 | tf_op jit(solution)/shard_map/separator/all_to_all | solution.py:288
  130.3 4.0 %all-gather.3.cloned.1.call-done.whole_ref = f32[1024,256]{1,0:T(8,128)} async-done(((f32[64,256]{1,0:T(8,128)}), f32[1024,256]{1,0:T(8,128)}) %all-gather.3.cloned.1.call-update) | async-done | bytes 1048592 | tf_op jit(solution)/shard_map/front_gather/all_gather | solution.py:326
  134.3 5.1 %all-to-all-done.4.blocks_ref = f32[16,16,128]{2,1,0:T(8,128)S(1)} async-done(((f32[16,16,128]{2,1,0:T(8,128)}), f32[16,16,128]{2,1,0:T(8,128)S(1)}, u32[]{:S(2)}, u32[]{:S(2)}) %all-to-all-start.4) | async-done | bytes 131104 | tf_op jit(solution)/shard_map/separator/all_to_all | solution.py:288
  139.4 5.5 %final.1 = (f32[1,2,128,1024]{3,2,1,0:T(8,128)}, f32[32,1024]{1,0:T(8,128)}) custom-call(s32[2]{0:T(128)S(1)} %pad_add_fusion.me_ref, s32[32]{0:T(128)S(1)} %copy-done.7, f32[1024,256]{1,0:T(8,128)} %all-gather.3.cloned.1.call-done.whole_ref, f32[16,16,128]{2,1,0:T(8,128)S(1)} %all-to-all-done.4.blocks_ref, f32[1024,1024]{1,0:T(8,128)} %copy-done.1), custom_call_target="tpu_custom_call" | custom-call | tf_op jit(solution)/shard_map/final/final/pallas_call | solution.py:244
  (19 shorter events, 0.2 us)
Async XLA Ops:
  7.2 0.9 copy-start
  8.9 20.2 %all-to-all-start = ((f32[32,2,1024]{2,1,0:T(2,128)}), f32[32,2,1024]{2,1,0:T(2,128)S(1)}, u32[]{:S(2)}, u32[]{:S(2)}) async-start(f32[32,2,1024]{2,1,0:T(2,128)} %broadcast_in_dim.4), calls=%async_computation | async-start | bytes 524288 | tf_op jit(solution)/shard_map/factor_gather/all_to_all | solution.py:288
  19.4 66.4 %all-gather.5.cloned.1.call-start = ((), (), s32[]{:S(2)}) async-start(), calls=%async_computation.6 | async-start | bytes 2785280 | tf_op jit(solution)/shard_map/factor_gather/all_gather | solution.py:299
  20.3 0.7 copy-start.6
  30.2 104.1 %all-gather.3.cloned.1.call-start = ((), (), s32[]{:S(2)}) async-start(), calls=%async_computation.5 | async-start | bytes 1114112 | tf_op jit(solution)/shard_map/front_gather/all_gather | solution.py:326
  75.6 9.5 %collective-permute-start = (f32[64,256]{1,0:T(8,128)S(1)}, f32[64,256]{1,0:T(8,128)S(1)}, u32[]{:S(2)}, u32[]{:S(2)}) collective-permute-start(f32[64,256]{1,0:T(8,128)S(1)} %total.4), channel_id=1, source_target_pairs={{0,0},{1,16},{2,32},{3,48},{4,64},{5,80},{6,96},{7,112},{8,128},{9... | collective-permute-start | bytes 196616 | tf_op jit(solution)/shard_map/front_sum/ppermute | solution.py:324
  85.1 0.7 copy-start.4
  85.8 1.7 %copy-start.3 = (f32[320,16,128]{2,1,0:T(8,128)S(1)}, f32[320,16,128]{2,1,0:T(8,128)}, u32[]{:S(2)}) copy-start(f32[320,16,128]{2,1,0:T(8,128)} %all-gather.5.cloned.1.call-done) | copy-start | bytes 7864324
  87.5 6.7 %copy-start.2 = (f32[1,2,128,1024]{3,2,1,0:T(8,128)S(1)}, f32[1,2,128,1024]{3,2,1,0:T(8,128)}, u32[]{:S(2)}) copy-start(f32[1,2,128,1024]{3,2,1,0:T(8,128)} %panel_ref.3) | copy-start | bytes 3145732
  87.5 6.7 %copy-start.5 = (f32[64,256]{1,0:T(8,128)S(1)}, f32[64,256]{1,0:T(8,128)}, u32[]{:S(2)}) copy-start(f32[64,256]{1,0:T(8,128)} %copy-done.4) | copy-start | bytes 196612
  87.5 6.7 %copy-start.7 = (s32[32]{0:T(128)S(1)}, s32[32]{0:T(128)}, u32[]{:S(2)}) copy-start(s32[32]{0:T(128)} %count_ref.5) | copy-start | bytes 388
  94.2 2.0 %copy-start.1 = (f32[1024,1024]{1,0:T(8,128)}, f32[1024,1024]{1,0:T(8,128)S(1)}, u32[]{:S(2)}) copy-start(f32[1024,1024]{1,0:T(8,128)S(1)} %factor_inverse.1.inverse_ref) | copy-start | bytes 12582916
  120.9 18.5 %all-to-all-start.4 = ((f32[16,16,128]{2,1,0:T(8,128)}), f32[16,16,128]{2,1,0:T(8,128)S(1)}, u32[]{:S(2)}, u32[]{:S(2)}) async-start(f32[16,16,128]{2,1,0:T(8,128)} %broadcast_in_dim.5), calls=%async_computation.4 | async-start | bytes 262144 | tf_op jit(solution)/shard_map/separator/all_to_all | solution.py:288
Sparse Core Ops, SparseCore 0:
  30.3 46.2 all-gather.4
  85.9 48.3 all-gather.2

commit v5 on v4

--- a/solution.py
+++ b/solution.py
@@ -217,7 +217,7 @@
     )(me, slot_count, piece, panel, inverse)
 
 
-def final_kernel(me_ref, count_ref, whole_ref, blocks_ref, inverse_ref, update_ref, sep_ref, left_ref):
+def update_kernel(me_ref, count_ref, whole_ref, inverse_ref, update_ref, left_ref):
     @pl.when(pl.program_id(0) == 0)
     def _():
         row = me_ref[0]
@@ -225,44 +225,61 @@
         for slot in range(2):
             sign = -(slot < count_ref[row]).astype(jnp.float32)
             left_ref[slot * TILE : (slot + 1) * TILE, :] = turned[slot * TILE : (slot + 1) * TILE] * sign
-        for side in range(2):
-            lanes = slice(side * WIDTH, (side + 1) * WIDTH)
-            start = 2 * TILE + side * (OWN // 2)
-            left_ref[start : start + OWN // 2, :] = jnp.concatenate(
-                [blocks_ref[place][:, lanes] for place in range(N_COL)], axis=1
-            )
 
     @for_stripe
     def _(stripe):
         result = times_inverse(left_ref, inverse_ref, stripe)
         update_ref[0, 0] = result[:TILE]
-        update_ref[0, 1] = result[TILE : 2 * TILE]
-        sep_ref[...] = result[2 * TILE :]
-
-
-def final(me, slot_count, whole, blocks, inverse):
-    return pl.pallas_call(
-        final_kernel,
+        update_ref[0, 1] = result[TILE:]
+
+
+def update_rows(me, slot_count, whole, inverse):
+    return pl.pallas_call(
+        update_kernel,
         grid=(X,),
         in_specs=[
             SMEM,
             SMEM,
             whole_block((SEP, 2 * TILE)),
+            pl.BlockSpec((SEP, STRIPE), lambda i: (0, i)),
+        ],
+        out_specs=pl.BlockSpec((1, 2, TILE, STRIPE), lambda i: (0, 0, 0, i)),
+        out_shape=jax.ShapeDtypeStruct((1, 2, TILE, SEP), jnp.float32),
+        scratch_shapes=[pltpu.VMEM((2 * TILE, SEP), jnp.float32)],
+        compiler_params=pltpu.CompilerParams(vmem_limit_bytes=16 * MIB),
+        name="update_rows",
+    )(me, slot_count, off_chip(whole), off_chip(inverse))
+
+
+def separator_rows_kernel(blocks_ref, inverse_ref, sep_ref, left_ref):
+    @pl.when(pl.program_id(0) == 0)
+    def _():
+        for side in range(2):
+            lanes = slice(side * WIDTH, (side + 1) * WIDTH)
+            start = side * (OWN // 2)
+            left_ref[start : start + OWN // 2, :] = jnp.concatenate(
+                [blocks_ref[place][:, lanes] for place in range(N_COL)], axis=1
+            )
+
+    @for_stripe
+    def _(stripe):
+        sep_ref[...] = times_inverse(left_ref, inverse_ref, stripe)
+
+
+def separator_rows(blocks, inverse):
+    return pl.pallas_call(
+        separator_rows_kernel,
+        grid=(X,),
+        in_specs=[
             whole_block((N_COL, OWN // 2, 2 * WIDTH)),
             pl.BlockSpec((SEP, STRIPE), lambda i: (0, i)),
         ],
-        out_specs=(
-            pl.BlockSpec((1, 2, TILE, STRIPE), lambda i: (0, 0, 0, i)),
-            pl.BlockSpec((OWN, STRIPE), lambda i: (0, i)),
-        ),
-        out_shape=(
-            jax.ShapeDtypeStruct((1, 2, TILE, SEP), jnp.float32),
-            jax.ShapeDtypeStruct((OWN, SEP), jnp.float32),
-        ),
-        scratch_shapes=[pltpu.VMEM((2 * TILE + OWN, SEP), jnp.float32)],
-        compiler_params=pltpu.CompilerParams(vmem_limit_bytes=16 * MIB),
-        name="final",
-    )(me, slot_count, off_chip(whole), blocks, off_chip(inverse))
+        out_specs=pl.BlockSpec((OWN, STRIPE), lambda i: (0, i)),
+        out_shape=jax.ShapeDtypeStruct((OWN, SEP), jnp.float32),
+        scratch_shapes=[pltpu.VMEM((OWN, SEP), jnp.float32)],
+        compiler_params=pltpu.CompilerParams(vmem_limit_bytes=12 * MIB),
+        name="separator_rows",
+    )(blocks, off_chip(inverse))
 
 
 def total_kernel(pieces_ref, out_ref):
@@ -332,7 +349,7 @@
         taken = total(exchange(sent, ROW))
         blocks = exchange(lax.optimization_barrier(spread(taken, N_COL)), COL)
     with jax.named_scope("final"):
-        return final(me, slot_count, whole, blocks, inverse)
+        return update_rows(me, slot_count, whole, inverse), separator_rows(blocks, inverse)
 
 
 def solution(mesh):

time: 152 us -> 151 us (level)
  waiting for transfers between devices: 16.5 us -> 11.4 us
  Pallas kernels: 17.7 us -> 21.9 us
    all_to_all x2, waiting for transfers between devices: 9.82 us -> 4.68 us  [exchange(): return lax.all_to_all(blocks, axis, 0, 0, tiled=True)]
    pallas_call x1 -> x2, Pallas kernels: 5.47 us -> 9.69 us  [the longest x1 5.31 us: update_rows(): pl.pallas_call(update_kernel, grid=(X,), in_specs=[SMEM, SMEM, whole_bloc...]
  transfers between devices with their start and end apart: 5 -> 5, of which waited for: 4 -> 3; matrix products, arithmetic and copies ran while one was open for 1% -> 1% of each run, Pallas kernels for 8% -> 12%
where the time goes in v5:
time: 151 us
  blocking collectives  69.3 us (46%)
  starting transfers between devices  26.8 us (18%)
  Pallas kernels  21.9 us (15%)
  between operations  14.2 us (9%)
  waiting for transfers between devices  11.4 us (8%)
  local copies, waits for them, and re-layouts  7.14 us (5%)
    all_to_all x3, blocking collectives, exchange(): return lax.all_to_all(blocks, axis, 0, 0, tiled=True)  69.3 us
    all_to_all x2, starting transfers between devices, exchange(): return lax.all_to_all(blocks, axis, 0, 0, tiled=True)  19.9 us
    ppermute x1, starting transfers between devices, on_device(): piece = lax.ppermute(piece, ROW + COL, to_slot_owner())  6.84 us
    pallas_call x1, Pallas kernels, factor_inverse(): pl.pallas_call(inverse_kernel, in_specs=[VMEM], out_specs=VMEM, out_shape...  6.64 us
    pallas_call x1, Pallas kernels, update_rows(): pl.pallas_call(update_kernel, grid=(X,), in_specs=[SMEM, SMEM, whole_bloc...  5.31 us
    unnamed x17, local copies, waits for them, and re-layouts  4.71 us
    all_to_all x2, waiting for transfers between devices, exchange(): return lax.all_to_all(blocks, axis, 0, 0, tiled=True)  4.68 us
    pallas_call x1, Pallas kernels, separator_rows(): pl.pallas_call(separator_rows_kernel, grid=(X,), in_specs=[whole_block((N...  4.37 us
  transfers between devices with their start and end apart: 5, of which 3 were waited for; matrix products, arithmetic and copies ran while one was open for 1% of the time, Pallas kernels for 12%

profile of v5, /device:TPU:1, one launch (start us, length us, event | category | flops | bytes accessed | tf_op | source)
XLA Modules:
  0.0 150.8 jit_solution(10197256209121222322)
XLA Ops:
  7.2 0.0 copy-start
  7.2 0.9 copy-done
  8.1 0.8 broadcast_in_dim.4
  8.9 10.5 %all-to-all-start = ((f32[32,2,1024]{2,1,0:T(2,128)}), f32[32,2,1024]{2,1,0:T(2,128)S(1)}, u32[]{:S(2)}, u32[]{:S(2)}) async-start(f32[32,2,1024]{2,1,0:T(2,128)} %broadcast_in_dim.4), calls=%async_computation | async-start | bytes 524288 | tf_op jit(solution)/shard_map/factor_gather/all_to_all | solution.py:305
  19.4 0.0 all-gather.5.cloned.1.call-start
  19.4 0.8 copy.10.tile_ref
  20.2 0.1 pad_add_fusion.me_ref
  20.3 0.7 copy-done.6
  20.9 3.5 %front.1 = f32[2,1024,256]{2,1,0:T(8,128)S(1)} custom-call(s32[32,2]{1,0:T(8,128)S(1)} %copy.10.tile_ref, s32[32]{0:T(128)S(1)} %copy-done.6, s32[2]{0:T(128)S(1)} %pad_add_fusion.me_ref, f32[4,1024,128]{2,1,0:T(8,128)} %bitcast.21, f32[4,1024,128]{2,1,0:T(8,128)} %bitcast.22, f32[1,2,128,1024]{3,2,1,0:T(8,128)} %panel_ref.3), custom_call_target="tpu_custom_call" | custom-call | tf_op jit(solution)/shard_map/front_product/front/pallas_call | solution.py:75
  24.4 4.7 %all-to-all-done = f32[32,2,1024]{2,1,0:T(2,128)S(1)} async-done(((f32[32,2,1024]{2,1,0:T(2,128)}), f32[32,2,1024]{2,1,0:T(2,128)S(1)}, u32[]{:S(2)}, u32[]{:S(2)}) %all-to-all-start) | async-done | bytes 262176 | tf_op jit(solution)/shard_map/factor_gather/all_to_all | solution.py:305
  29.1 0.2 reshape.26
  29.3 0.1 squeeze.15
  29.4 0.7 copy.11
  30.1 0.0 all-gather.5.cloned.1.call-update
  30.2 0.0 all-gather.3.cloned.1.call-start
  30.2 25.1 %all_to_all.25.pieces_ref = f32[4,8,64,256]{3,2,1,0:T(8,128)S(1)} all-to-all(f32[4,8,64,256]{3,2,1,0:T(8,128)S(1)} %bitcast.19), channel_id=1, replica_groups=mesh['x'=4,'y'=8,'z'=8,'core'=2] {'x'}, dimensions={0} | all-to-all | bytes 4194304 | tf_op jit(solution)/shard_map/front_sum/all_to_all | solution.py:305
  55.3 0.1 total.3
  55.4 20.2 %all_to_all.26.pieces_ref = f32[8,64,256]{2,1,0:T(8,128)S(1)} all-to-all(f32[8,64,256]{2,1,0:T(8,128)S(1)} %total.3), channel_id=1, replica_groups=mesh['x'=4,'y'=8,'z'=8,'core'=2] {'y'}, dimensions={0} | all-to-all | bytes 1048576 | tf_op jit(solution)/shard_map/front_sum/all_to_all | solution.py:305
  75.6 6.8 %collective-permute-start = (f32[64,256]{1,0:T(8,128)S(1)}, f32[64,256]{1,0:T(8,128)S(1)}, u32[]{:S(2)}, u32[]{:S(2)}) collective-permute-start(f32[64,256]{1,0:T(8,128)S(1)} %total.4), channel_id=1, source_target_pairs={{0,0},{1,16},{2,32},{3,48},{4,64},{5,80},{6,96},{7,112},{8,128},{9... | collective-permute-start | bytes 196616 | tf_op jit(solution)/shard_map/front_sum/ppermute | solution.py:341
  82.5 2.6 %collective-permute-done.piece_ref = f32[64,256]{1,0:T(8,128)S(1)} collective-permute-done((f32[64,256]{1,0:T(8,128)S(1)}, f32[64,256]{1,0:T(8,128)S(1)}, u32[]{:S(2)}, u32[]{:S(2)}) %collective-permute-start) | collective-permute-done | bytes 65568 | tf_op jit(solution)/shard_map/front_sum/ppermute | solution.py:341
  85.1 0.7 copy-done.4
  85.7 0.0 all-gather.3.cloned.1.call-update
  85.8 0.0 all-gather.5.cloned.1.call-done
  85.8 1.7 %copy-done.3 = f32[320,16,128]{2,1,0:T(8,128)S(1)} copy-done((f32[320,16,128]{2,1,0:T(8,128)S(1)}, f32[320,16,128]{2,1,0:T(8,128)}, u32[]{:S(2)}) %copy-start.3) | copy-done | bytes 2621464
  87.5 6.6 %factor_inverse.1.inverse_ref = f32[1024,1024]{1,0:T(8,128)S(1)} custom-call(f32[5120,128]{1,0:T(8,128)S(1)} %bitcast.20), custom_call_target="tpu_custom_call" | custom-call | tf_op jit(solution)/shard_map/inverse/factor_inverse/pallas_call | solution.py:166
  94.2 1.9 %separator.1 = f32[32,16,128]{2,1,0:T(8,128)S(1)} custom-call(s32[2]{0:T(128)S(1)} %pad_add_fusion.me_ref, s32[32]{0:T(128)S(1)} %copy-done.7, f32[64,256]{1,0:T(8,128)S(1)} %copy-done.5, f32[1,2,128,1024]{3,2,1,0:T(8,128)S(1)} %copy-done.2, f32[1024,1024]{1,0:T(8,128)S(1)} %factor_inverse.1.inverse_ref), custom_call_target="tpu_custom_call" | custom-call | tf_op jit(solution)/shard_map/separator/separator/pallas_call | solution.py:210
  96.2 24.0 %all_to_all.27.pieces_ref = f32[32,16,128]{2,1,0:T(8,128)S(1)} all-to-all(f32[32,16,128]{2,1,0:T(8,128)S(1)} %separator.1), channel_id=1, replica_groups=mesh['x'=4,'y'=8,'z'=8,'core'=2] {'x','y'}, dimensions={0} | all-to-all | bytes 524288 | tf_op jit(solution)/shard_map/separator/all_to_all | solution.py:305
  120.2 0.7 broadcast_in_dim.5
  120.9 9.4 %all-to-all-start.4 = ((f32[16,16,128]{2,1,0:T(8,128)}), f32[16,16,128]{2,1,0:T(8,128)S(1)}, u32[]{:S(2)}, u32[]{:S(2)}) async-start(f32[16,16,128]{2,1,0:T(8,128)} %broadcast_in_dim.5), calls=%async_computation.4 | async-start | bytes 262144 | tf_op jit(solution)/shard_map/separator/all_to_all | solution.py:305
  130.3 4.0 %all-gather.3.cloned.1.call-done.whole_ref = f32[1024,256]{1,0:T(8,128)} async-done(((f32[64,256]{1,0:T(8,128)}), f32[1024,256]{1,0:T(8,128)}) %all-gather.3.cloned.1.call-update) | async-done | bytes 1048592 | tf_op jit(solution)/shard_map/front_gather/all_gather | solution.py:343
  134.3 5.3 %update_rows.1 = f32[1,2,128,1024]{3,2,1,0:T(8,128)} custom-call(s32[2]{0:T(128)S(1)} %pad_add_fusion.me_ref, s32[32]{0:T(128)S(1)} %copy-done.7, f32[1024,256]{1,0:T(8,128)} %all-gather.3.cloned.1.call-done.whole_ref, f32[1024,1024]{1,0:T(8,128)} %copy-done.1), custom_call_target="tpu_custom_call" | custom-call | tf_op jit(solution)/shard_map/final/update_rows/pallas_call | solution.py:237
  139.6 4.4 %separator_rows.1 = f32[32,1024]{1,0:T(8,128)} custom-call(f32[16,16,128]{2,1,0:T(8,128)S(1)} %all-to-all-done.4.blocks_ref, f32[1024,1024]{1,0:T(8,128)} %copy-done.1), custom_call_target="tpu_custom_call" | custom-call | tf_op jit(solution)/shard_map/final/separator_rows/pallas_call | solution.py:270
  (20 shorter events, 0.2 us)
Async XLA Ops:
  7.2 0.9 copy-start
  8.9 20.2 %all-to-all-start = ((f32[32,2,1024]{2,1,0:T(2,128)}), f32[32,2,1024]{2,1,0:T(2,128)S(1)}, u32[]{:S(2)}, u32[]{:S(2)}) async-start(f32[32,2,1024]{2,1,0:T(2,128)} %broadcast_in_dim.4), calls=%async_computation | async-start | bytes 524288 | tf_op jit(solution)/shard_map/factor_gather/all_to_all | solution.py:305
  19.4 66.4 %all-gather.5.cloned.1.call-start = ((), (), s32[]{:S(2)}) async-start(), calls=%async_computation.6 | async-start | bytes 2785280 | tf_op jit(solution)/shard_map/factor_gather/all_gather | solution.py:316
  20.3 0.7 copy-start.6
  30.2 104.1 %all-gather.3.cloned.1.call-start = ((), (), s32[]{:S(2)}) async-start(), calls=%async_computation.5 | async-start | bytes 1114112 | tf_op jit(solution)/shard_map/front_gather/all_gather | solution.py:343
  75.6 9.5 %collective-permute-start = (f32[64,256]{1,0:T(8,128)S(1)}, f32[64,256]{1,0:T(8,128)S(1)}, u32[]{:S(2)}, u32[]{:S(2)}) collective-permute-start(f32[64,256]{1,0:T(8,128)S(1)} %total.4), channel_id=1, source_target_pairs={{0,0},{1,16},{2,32},{3,48},{4,64},{5,80},{6,96},{7,112},{8,128},{9... | collective-permute-start | bytes 196616 | tf_op jit(solution)/shard_map/front_sum/ppermute | solution.py:341
  85.1 0.7 copy-start.4
  85.8 1.7 %copy-start.3 = (f32[320,16,128]{2,1,0:T(8,128)S(1)}, f32[320,16,128]{2,1,0:T(8,128)}, u32[]{:S(2)}) copy-start(f32[320,16,128]{2,1,0:T(8,128)} %all-gather.5.cloned.1.call-done) | copy-start | bytes 7864324
  87.5 6.7 %copy-start.2 = (f32[1,2,128,1024]{3,2,1,0:T(8,128)S(1)}, f32[1,2,128,1024]{3,2,1,0:T(8,128)}, u32[]{:S(2)}) copy-start(f32[1,2,128,1024]{3,2,1,0:T(8,128)} %panel_ref.3) | copy-start | bytes 3145732
  87.5 6.7 %copy-start.5 = (f32[64,256]{1,0:T(8,128)S(1)}, f32[64,256]{1,0:T(8,128)}, u32[]{:S(2)}) copy-start(f32[64,256]{1,0:T(8,128)} %copy-done.4) | copy-start | bytes 196612
  87.5 6.7 %copy-start.7 = (s32[32]{0:T(128)S(1)}, s32[32]{0:T(128)}, u32[]{:S(2)}) copy-start(s32[32]{0:T(128)} %count_ref.5) | copy-start | bytes 388
  94.2 2.0 %copy-start.1 = (f32[1024,1024]{1,0:T(8,128)}, f32[1024,1024]{1,0:T(8,128)S(1)}, u32[]{:S(2)}) copy-start(f32[1024,1024]{1,0:T(8,128)S(1)} %factor_inverse.1.inverse_ref) | copy-start | bytes 12582916
  120.9 18.7 %all-to-all-start.4 = ((f32[16,16,128]{2,1,0:T(8,128)}), f32[16,16,128]{2,1,0:T(8,128)S(1)}, u32[]{:S(2)}, u32[]{:S(2)}) async-start(f32[16,16,128]{2,1,0:T(8,128)} %broadcast_in_dim.5), calls=%async_computation.4 | async-start | bytes 262144 | tf_op jit(solution)/shard_map/separator/all_to_all | solution.py:305
Sparse Core Ops, SparseCore 0:
  30.3 46.2 all-gather.4
  85.9 48.3 all-gather.2

commit v6 on v5

--- a/solution.py
+++ b/solution.py
@@ -251,32 +251,35 @@
     )(me, slot_count, off_chip(whole), off_chip(inverse))
 
 
-def separator_rows_kernel(blocks_ref, inverse_ref, sep_ref, left_ref):
-    @pl.when(pl.program_id(0) == 0)
-    def _():
-        for side in range(2):
-            lanes = slice(side * WIDTH, (side + 1) * WIDTH)
-            start = side * (OWN // 2)
-            left_ref[start : start + OWN // 2, :] = jnp.concatenate(
-                [blocks_ref[place][:, lanes] for place in range(N_COL)], axis=1
-            )
-
-    @for_stripe
-    def _(stripe):
-        sep_ref[...] = times_inverse(left_ref, inverse_ref, stripe)
+def separator_rows_kernel(blocks_ref, inverse_ref, sep_ref, held_ref, arrived):
+    def rows(stripe):
+        return pl.ds(stripe * STRIPE, STRIPE), pl.ds(0, (stripe + 1) * STRIPE)
+
+    copies = [
+        pltpu.make_async_copy(inverse_ref.at[rows(stripe)], held_ref.at[rows(stripe)], arrived.at[stripe])
+        for stripe in range(X)
+    ]
+    for copy in reversed(copies):
+        copy.start()
+    blocks = [blocks_ref[place] for place in range(N_COL)]
+    sides = [
+        jnp.concatenate([block[:, side * WIDTH : (side + 1) * WIDTH] for block in blocks], axis=1) for side in range(2)
+    ]
+    left = jnp.concatenate(sides, axis=0)
+    for stripe in reversed(range(X)):
+        copies[stripe].wait()
+        first = stripe * STRIPE
+        lanes = slice(first, first + STRIPE)
+        sep_ref[:, lanes] = fine_dot(left[:, first:], held_ref[first:, lanes])
 
 
 def separator_rows(blocks, inverse):
     return pl.pallas_call(
         separator_rows_kernel,
-        grid=(X,),
-        in_specs=[
-            whole_block((N_COL, OWN // 2, 2 * WIDTH)),
-            pl.BlockSpec((SEP, STRIPE), lambda i: (0, i)),
-        ],
-        out_specs=pl.BlockSpec((OWN, STRIPE), lambda i: (0, i)),
+        in_specs=[VMEM, pl.BlockSpec(memory_space=pl.ANY)],
+        out_specs=VMEM,
         out_shape=jax.ShapeDtypeStruct((OWN, SEP), jnp.float32),
-        scratch_shapes=[pltpu.VMEM((OWN, SEP), jnp.float32)],
+        scratch_shapes=[pltpu.VMEM((SEP, SEP), jnp.float32), pltpu.SemaphoreType.DMA((X,))],
         compiler_params=pltpu.CompilerParams(vmem_limit_bytes=12 * MIB),
         name="separator_rows",
     )(blocks, off_chip(inverse))

time: 151 us -> 150 us (level)
  no operation moved by 1% of the time
where the time goes in v6:
time: 150 us
  blocking collectives  69.2 us (46%)
  starting transfers between devices  26.8 us (18%)
  Pallas kernels  20.9 us (14%)
  between operations  14.2 us (9%)
  waiting for transfers between devices  11.4 us (8%)
  local copies, waits for them, and re-layouts  7.14 us (5%)
    all_to_all x3, blocking collectives, exchange(): return lax.all_to_all(blocks, axis, 0, 0, tiled=True)  69.2 us
    all_to_all x2, starting transfers between devices, exchange(): return lax.all_to_all(blocks, axis, 0, 0, tiled=True)  19.9 us
    ppermute x1, starting transfers between devices, on_device(): piece = lax.ppermute(piece, ROW + COL, to_slot_owner())  6.84 us
    pallas_call x1, Pallas kernels, factor_inverse(): pl.pallas_call(inverse_kernel, in_specs=[VMEM], out_specs=VMEM, out_shape...  6.65 us
    pallas_call x1, Pallas kernels, update_rows(): pl.pallas_call(update_kernel, grid=(X,), in_specs=[SMEM, SMEM, whole_bloc...  5.31 us
    unnamed x17, local copies, waits for them, and re-layouts  4.71 us
    all_to_all x2, waiting for transfers between devices, exchange(): return lax.all_to_all(blocks, axis, 0, 0, tiled=True)  4.69 us
    all_gather x1, waiting for transfers between devices, on_device(): whole = lax.all_gather(piece, COL, axis=0, tiled=True)  4.02 us
  transfers between devices with their start and end apart: 5, of which 3 were waited for; matrix products, arithmetic and copies ran while one was open for 1% of the time, Pallas kernels for 12%

profile of v6, /device:TPU:1, one launch (start us, length us, event | category | flops | bytes accessed | tf_op | source)
XLA Modules:
  0.0 149.8 jit_solution(13892406240941685842)
XLA Ops:
  7.2 0.0 copy-start
  7.2 0.9 copy-done
  8.1 0.8 broadcast_in_dim.4
  8.9 10.5 %all-to-all-start = ((f32[32,2,1024]{2,1,0:T(2,128)}), f32[32,2,1024]{2,1,0:T(2,128)S(1)}, u32[]{:S(2)}, u32[]{:S(2)}) async-start(f32[32,2,1024]{2,1,0:T(2,128)} %broadcast_in_dim.4), calls=%async_computation | async-start | bytes 524288 | tf_op jit(solution)/shard_map/factor_gather/all_to_all | solution.py:308
  19.4 0.0 all-gather.5.cloned.1.call-start
  19.4 0.8 copy.10.tile_ref
  20.2 0.1 pad_add_fusion.me_ref
  20.3 0.7 copy-done.6
  20.9 3.4 %front.1 = f32[2,1024,256]{2,1,0:T(8,128)S(1)} custom-call(s32[32,2]{1,0:T(8,128)S(1)} %copy.10.tile_ref, s32[32]{0:T(128)S(1)} %copy-done.6, s32[2]{0:T(128)S(1)} %pad_add_fusion.me_ref, f32[4,1024,128]{2,1,0:T(8,128)} %bitcast.21, f32[4,1024,128]{2,1,0:T(8,128)} %bitcast.22, f32[1,2,128,1024]{3,2,1,0:T(8,128)} %panel_ref.3), custom_call_target="tpu_custom_call" | custom-call | tf_op jit(solution)/shard_map/front_product/front/pallas_call | solution.py:75
  24.4 4.7 %all-to-all-done = f32[32,2,1024]{2,1,0:T(2,128)S(1)} async-done(((f32[32,2,1024]{2,1,0:T(2,128)}), f32[32,2,1024]{2,1,0:T(2,128)S(1)}, u32[]{:S(2)}, u32[]{:S(2)}) %all-to-all-start) | async-done | bytes 262176 | tf_op jit(solution)/shard_map/factor_gather/all_to_all | solution.py:308
  29.1 0.2 reshape.26
  29.3 0.1 squeeze.15
  29.4 0.7 copy.11
  30.1 0.0 all-gather.5.cloned.1.call-update
  30.2 0.0 all-gather.3.cloned.1.call-start
  30.2 25.1 %all_to_all.25.pieces_ref = f32[4,8,64,256]{3,2,1,0:T(8,128)S(1)} all-to-all(f32[4,8,64,256]{3,2,1,0:T(8,128)S(1)} %bitcast.19), channel_id=1, replica_groups=mesh['x'=4,'y'=8,'z'=8,'core'=2] {'x'}, dimensions={0} | all-to-all | bytes 4194304 | tf_op jit(solution)/shard_map/front_sum/all_to_all | solution.py:308
  55.3 0.1 total.3
  55.4 20.2 %all_to_all.26.pieces_ref = f32[8,64,256]{2,1,0:T(8,128)S(1)} all-to-all(f32[8,64,256]{2,1,0:T(8,128)S(1)} %total.3), channel_id=1, replica_groups=mesh['x'=4,'y'=8,'z'=8,'core'=2] {'y'}, dimensions={0} | all-to-all | bytes 1048576 | tf_op jit(solution)/shard_map/front_sum/all_to_all | solution.py:308
  75.6 6.8 %collective-permute-start = (f32[64,256]{1,0:T(8,128)S(1)}, f32[64,256]{1,0:T(8,128)S(1)}, u32[]{:S(2)}, u32[]{:S(2)}) collective-permute-start(f32[64,256]{1,0:T(8,128)S(1)} %total.4), channel_id=1, source_target_pairs={{0,0},{1,16},{2,32},{3,48},{4,64},{5,80},{6,96},{7,112},{8,128},{9... | collective-permute-start | bytes 196616 | tf_op jit(solution)/shard_map/front_sum/ppermute | solution.py:344
  82.5 2.6 %collective-permute-done.piece_ref = f32[64,256]{1,0:T(8,128)S(1)} collective-permute-done((f32[64,256]{1,0:T(8,128)S(1)}, f32[64,256]{1,0:T(8,128)S(1)}, u32[]{:S(2)}, u32[]{:S(2)}) %collective-permute-start) | collective-permute-done | bytes 65568 | tf_op jit(solution)/shard_map/front_sum/ppermute | solution.py:344
  85.1 0.7 copy-done.4
  85.7 0.0 all-gather.3.cloned.1.call-update
  85.8 0.0 all-gather.5.cloned.1.call-done
  85.8 1.7 %copy-done.3 = f32[320,16,128]{2,1,0:T(8,128)S(1)} copy-done((f32[320,16,128]{2,1,0:T(8,128)S(1)}, f32[320,16,128]{2,1,0:T(8,128)}, u32[]{:S(2)}) %copy-start.3) | copy-done | bytes 2621464
  87.5 6.6 %factor_inverse.1.inverse_ref = f32[1024,1024]{1,0:T(8,128)S(1)} custom-call(f32[5120,128]{1,0:T(8,128)S(1)} %bitcast.20), custom_call_target="tpu_custom_call" | custom-call | tf_op jit(solution)/shard_map/inverse/factor_inverse/pallas_call | solution.py:166
  94.2 1.9 %separator.1 = f32[32,16,128]{2,1,0:T(8,128)S(1)} custom-call(s32[2]{0:T(128)S(1)} %pad_add_fusion.me_ref, s32[32]{0:T(128)S(1)} %copy-done.7, f32[64,256]{1,0:T(8,128)S(1)} %copy-done.5, f32[1,2,128,1024]{3,2,1,0:T(8,128)S(1)} %copy-done.2, f32[1024,1024]{1,0:T(8,128)S(1)} %factor_inverse.1.inverse_ref), custom_call_target="tpu_custom_call" | custom-call | tf_op jit(solution)/shard_map/separator/separator/pallas_call | solution.py:210
  96.2 24.0 %all_to_all.27.pieces_ref = f32[32,16,128]{2,1,0:T(8,128)S(1)} all-to-all(f32[32,16,128]{2,1,0:T(8,128)S(1)} %separator.1), channel_id=1, replica_groups=mesh['x'=4,'y'=8,'z'=8,'core'=2] {'x','y'}, dimensions={0} | all-to-all | bytes 524288 | tf_op jit(solution)/shard_map/separator/all_to_all | solution.py:308
  120.2 0.7 broadcast_in_dim.5
  120.9 9.4 %all-to-all-start.4 = ((f32[16,16,128]{2,1,0:T(8,128)}), f32[16,16,128]{2,1,0:T(8,128)S(1)}, u32[]{:S(2)}, u32[]{:S(2)}) async-start(f32[16,16,128]{2,1,0:T(8,128)} %broadcast_in_dim.5), calls=%async_computation.4 | async-start | bytes 262144 | tf_op jit(solution)/shard_map/separator/all_to_all | solution.py:308
  130.3 4.0 %all-gather.3.cloned.1.call-done.whole_ref = f32[1024,256]{1,0:T(8,128)} async-done(((f32[64,256]{1,0:T(8,128)}), f32[1024,256]{1,0:T(8,128)}) %all-gather.3.cloned.1.call-update) | async-done | bytes 1048592 | tf_op jit(solution)/shard_map/front_gather/all_gather | solution.py:346
  134.3 5.3 %update_rows.1 = f32[1,2,128,1024]{3,2,1,0:T(8,128)} custom-call(s32[2]{0:T(128)S(1)} %pad_add_fusion.me_ref, s32[32]{0:T(128)S(1)} %copy-done.7, f32[1024,256]{1,0:T(8,128)} %all-gather.3.cloned.1.call-done.whole_ref, f32[1024,1024]{1,0:T(8,128)} %copy-done.1), custom_call_target="tpu_custom_call" | custom-call | tf_op jit(solution)/shard_map/final/update_rows/pallas_call | solution.py:237
  139.6 3.3 %separator_rows.1 = f32[32,1024]{1,0:T(8,128)} custom-call(f32[16,16,128]{2,1,0:T(8,128)S(1)} %all-to-all-done.4.blocks_ref, f32[1024,1024]{1,0:T(8,128)} %copy-done.1), custom_call_target="tpu_custom_call" | custom-call | tf_op jit(solution)/shard_map/final/separator_rows/pallas_call | solution.py:277
  (20 shorter events, 0.2 us)
Async XLA Ops:
  7.2 0.9 copy-start
  8.9 20.2 %all-to-all-start = ((f32[32,2,1024]{2,1,0:T(2,128)}), f32[32,2,1024]{2,1,0:T(2,128)S(1)}, u32[]{:S(2)}, u32[]{:S(2)}) async-start(f32[32,2,1024]{2,1,0:T(2,128)} %broadcast_in_dim.4), calls=%async_computation | async-start | bytes 524288 | tf_op jit(solution)/shard_map/factor_gather/all_to_all | solution.py:308
  19.4 66.4 %all-gather.5.cloned.1.call-start = ((), (), s32[]{:S(2)}) async-start(), calls=%async_computation.6 | async-start | bytes 2785280 | tf_op jit(solution)/shard_map/factor_gather/all_gather | solution.py:319
  20.3 0.7 copy-start.6
  30.2 104.1 %all-gather.3.cloned.1.call-start = ((), (), s32[]{:S(2)}) async-start(), calls=%async_computation.5 | async-start | bytes 1114112 | tf_op jit(solution)/shard_map/front_gather/all_gather | solution.py:346
  75.6 9.5 %collective-permute-start = (f32[64,256]{1,0:T(8,128)S(1)}, f32[64,256]{1,0:T(8,128)S(1)}, u32[]{:S(2)}, u32[]{:S(2)}) collective-permute-start(f32[64,256]{1,0:T(8,128)S(1)} %total.4), channel_id=1, source_target_pairs={{0,0},{1,16},{2,32},{3,48},{4,64},{5,80},{6,96},{7,112},{8,128},{9... | collective-permute-start | bytes 196616 | tf_op jit(solution)/shard_map/front_sum/ppermute | solution.py:344
  85.1 0.7 copy-start.4
  85.8 1.7 %copy-start.3 = (f32[320,16,128]{2,1,0:T(8,128)S(1)}, f32[320,16,128]{2,1,0:T(8,128)}, u32[]{:S(2)}) copy-start(f32[320,16,128]{2,1,0:T(8,128)} %all-gather.5.cloned.1.call-done) | copy-start | bytes 7864324
  87.5 6.7 %copy-start.2 = (f32[1,2,128,1024]{3,2,1,0:T(8,128)S(1)}, f32[1,2,128,1024]{3,2,1,0:T(8,128)}, u32[]{:S(2)}) copy-start(f32[1,2,128,1024]{3,2,1,0:T(8,128)} %panel_ref.3) | copy-start | bytes 3145732
  87.5 6.7 %copy-start.5 = (f32[64,256]{1,0:T(8,128)S(1)}, f32[64,256]{1,0:T(8,128)}, u32[]{:S(2)}) copy-start(f32[64,256]{1,0:T(8,128)} %copy-done.4) | copy-start | bytes 196612
  87.5 6.7 %copy-start.7 = (s32[32]{0:T(128)S(1)}, s32[32]{0:T(128)}, u32[]{:S(2)}) copy-start(s32[32]{0:T(128)} %count_ref.5) | copy-start | bytes 388
  94.2 2.0 %copy-start.1 = (f32[1024,1024]{1,0:T(8,128)}, f32[1024,1024]{1,0:T(8,128)S(1)}, u32[]{:S(2)}) copy-start(f32[1024,1024]{1,0:T(8,128)S(1)} %factor_inverse.1.inverse_ref) | copy-start | bytes 12582916
  120.9 18.7 %all-to-all-start.4 = ((f32[16,16,128]{2,1,0:T(8,128)}), f32[16,16,128]{2,1,0:T(8,128)S(1)}, u32[]{:S(2)}, u32[]{:S(2)}) async-start(f32[16,16,128]{2,1,0:T(8,128)} %broadcast_in_dim.5), calls=%async_computation.4 | async-start | bytes 262144 | tf_op jit(solution)/shard_map/separator/all_to_all | solution.py:308
Sparse Core Ops, SparseCore 0:
  30.3 46.2 all-gather.4
  85.9 48.3 all-gather.2
